TPU v7x, 32 devices: a whole 2x2x4 slice. The times are simulated.
32 devices in a mesh: row: 4 (over y, x), col: 8 (over z, core).
Axes of the slice: x: 2, y: 2, z: 4, core: 2. Of those that a mesh axis runs over, the one named last changes fastest.
Arguments:
- panel_right: bfloat16 [32, 1536, 128], P('row', 'col'), may hold values from -1 to 1
- factor_inverse: bfloat16 [1536, 1536], replicated, as said below
- ranks: int32 [32], P(('row', 'col')), may hold values from 32 to 128
- owner_map: int32 [32], replicated, may hold values from 0 to 31, each once
- cores: float32 [4, 8, 8, 4, 128, 128], P('row', 'col'), may hold values from -6 to 6
Outputs:
- new_cores: float32 [4, 8, 8, 4, 128, 128], P('row', 'col')
Inputs may be any that keep to these rules, and one draw needn't show every extreme that they name: `factor_inverse`: lower triangular, the inverse of a Cholesky factor.
All inputs are finite; a program needn't handle non-finite values.
Results may differ from a plain program's by a relative error of at most 0.0033.
Values may be sent and summed in bfloat16 or wider, within the bound.
No kernel may reach another device: no remote copies, remote signals or barrier semaphores. Data moves between devices by JAX's collectives and lax.ppermute only.
A program may use at most 128 MiB of HBM per device.

v0:
```python
import jax
import jax.numpy as jnp
from jax import lax
from jax.sharding import PartitionSpec as P


def body(panel_right, factor_inverse, ranks, owner_map, cores):
    n_row = lax.axis_size("row")
    n_col = lax.axis_size("col")
    devices = n_row * n_col
    order = factor_inverse.shape[0]
    width = panel_right.shape[2]
    whole = lax.all_to_all(panel_right, "col", split_axis=0, concat_axis=1, tiled=True)
    solved = jnp.einsum("ij,bjk->bik", factor_inverse, whole, preferred_element_type=jnp.float32)
    column = lax.broadcasted_iota(jnp.int32, (1, 1, width), 2)
    keep = column < ranks.reshape(1, 1, 1)
    panel_left = jnp.where(keep, solved, 0.0).astype(jnp.bfloat16)
    pieces = panel_left.reshape(devices, order // devices, width)
    spread = lax.all_to_all(pieces, ("row", "col"), split_axis=0, concat_axis=0, tiled=True)
    moved = jnp.take(spread, owner_map, axis=0)
    back = lax.all_to_all(moved, ("row", "col"), split_axis=0, concat_axis=0, tiled=True)
    held = back.reshape(1, order, width)
    column_set = lax.all_gather(held, "row", axis=0, tiled=True)
    gram = jnp.einsum(
        "aik,bil->abkl",
        lax.all_gather(held, "col", axis=0, tiled=True),
        column_set,
        preferred_element_type=jnp.float32,
    )
    return cores - gram[None, None]


def solution(mesh):
    return jax.shard_map(
        body,
        mesh=mesh,
        in_specs=(
            P("row", "col", None),
            P(),
            P(("row", "col")),
            P(),
            P("row", "col", None, None, None, None),
        ),
        out_specs=P("row", "col", None, None, None, None),
        check_vma=False,
    )
```

profile of v0, /device:TPU:0, one launch (start us, length us, event | category | flops | bytes accessed | tf_op | source)
XLA Modules:
  0.0 147.6 jit_solution(1991811806430617758)
XLA Ops:
  6.5 6.4 %all-to-all-start = ((bf16[8,192,128]{2,1,0:T(8,128)(2,1)}), bf16[8,192,128]{2,1,0:T(8,128)(2,1)S(1)}, u32[]{:S(2)}, u32[]{:S(2)}) async-start(bf16[8,192,128]{2,1,0:T(8,128)(2,1)} %param.5), calls=%async_computation | async-start | bytes 786432 | tf_op jit(solution)/shard_map/all_to_all | solution.py:13
  13.6 11.9 %all-to-all-done = bf16[8,192,128]{2,1,0:T(8,128)(2,1)S(1)} async-done(((bf16[8,192,128]{2,1,0:T(8,128)(2,1)}), bf16[8,192,128]{2,1,0:T(8,128)(2,1)S(1)}, u32[]{:S(2)}, u32[]{:S(2)}) %all-to-all-start) | async-done | bytes 393248 | tf_op jit(solution)/shard_map/all_to_all | solution.py:13
  25.4 0.0 copy-start
  25.4 4.0 %fusion.4 = bf16[1,1536,128]{1,2,0:T(8,128)(2,1)S(1)} fusion(bf16[1536,128]{1,0:T(8,128)(2,1)S(1)} %bitcast.33, bf16[1536,1536]{1,0:T(8,128)(2,1)} %param.6, pred[128]{0:T(512)(128)(4,1)S(1)} %iota_compare_fusion), kind=kOutput, calls=%fused_computation.6 | convolution fusion | flops 604372992 | bytes 5505152 | tf_op jit(solution)/shard_map/ij,bjk->bik/dot_general | solution.py:14
  29.4 0.9 copy.14
  30.4 3.5 %all-to-all-start.1 = ((bf16[32,48,128]{2,1,0:T(8,128)(2,1)}), bf16[32,48,128]{2,1,0:T(8,128)(2,1)S(1)}, u32[]{:S(2)}, u32[]{:S(2)}) async-start(bf16[32,48,128]{2,1,0:T(8,128)(2,1)} %bitcast.4), calls=%async_computation.1 | async-start | bytes 786432 | tf_op jit(solution)/shard_map/all_to_all | solution.py:19
  33.9 0.0 all-gather.3.cloned.1.call-start
  34.0 0.0 copy-done
  34.0 13.3 %all-to-all-done.1 = bf16[32,48,128]{2,1,0:T(8,128)(2,1)S(1)} async-done(((bf16[32,48,128]{2,1,0:T(8,128)(2,1)}), bf16[32,48,128]{2,1,0:T(8,128)(2,1)S(1)}, u32[]{:S(2)}, u32[]{:S(2)}) %all-to-all-start.1) | async-done | bytes 393248 | tf_op jit(solution)/shard_map/all_to_all | solution.py:19
  47.3 0.6 gather_fusion
  48.0 0.1 broadcast_select_fusion
  48.1 15.8 %all_to_all.19 = bf16[32,48,128]{2,1,0:T(8,128)(2,1)} all-to-all(bf16[32,48,128]{2,1,0:T(8,128)(2,1)S(1)} %broadcast_select_fusion), channel_id=1, replica_groups=mesh['row'=4,'col'=8] {'row','col'}, dimensions={0} | all-to-all | bytes 786432 | tf_op jit(solution)/shard_map/all_to_all | solution.py:21
  63.9 0.0 all-gather.3.cloned.1.call-update
  63.9 0.0 all-gather.5.cloned.1.call-start
  64.0 0.7 all-gather.5.cloned.1.call-update
  64.7 1.9 %copy.16 = f32[1,1,8,4,128,128]{4,5,2,3,1,0:T(8,128)S(1)} copy(f32[1,1,8,4,128,128]{5,4,3,2,1,0:T(8,128)} %param.9) | data formatting | bytes 4194304 | tf_op args[4]
  66.6 25.9 %all-gather.3.cloned.1.call-done = bf16[4,1536,128]{2,1,0:T(8,128)(2,1)} async-done(((bf16[1,1536,128]{2,1,0:T(8,128)(2,1)}), bf16[4,1536,128]{2,1,0:T(8,128)(2,1)}) %all-gather.3.cloned.1.call-update) | async-done | bytes 1572880 | tf_op jit(solution)/shard_map/all_gather | solution.py:23
  92.5 39.9 %all-gather.5.cloned.1.call-done = bf16[8,1536,128]{2,1,0:T(8,128)(2,1)} async-done(((bf16[1,1536,128]{2,1,0:T(8,128)(2,1)}), bf16[8,1536,128]{2,1,0:T(8,128)(2,1)}) %all-gather.5.cloned.1.call-update) | async-done | bytes 3145744 | tf_op jit(solution)/shard_map/all_gather | solution.py:26
  132.4 5.5 %bitcast_subtract_fusion = f32[1,1,8,4,128,128]{4,5,2,3,1,0:T(8,128)} fusion(f32[1,1,8,4,128,128]{4,5,2,3,1,0:T(8,128)S(1)} %copy.16, bf16[8,1536,128]{2,1,0:T(8,128)(2,1)} %all-gather.5.cloned.1.call-done, bf16[4,1536,128]{2,1,0:T(8,128)(2,1)} %all-gather.3.cloned.1.call-done), kind=kOutput, calls=%fused_computation.7 | convolution fusion | flops 1611137024 | bytes 8912896 | tf_op jit(solution)/shard_map/aik,bil->abkl/dot_general | solution.py:24
  137.9 2.9 %copy.17 = f32[1,1,8,4,128,128]{5,4,3,2,1,0:T(8,128)} copy(f32[1,1,8,4,128,128]{4,5,2,3,1,0:T(8,128)} %bitcast_subtract_fusion) | data formatting | bytes 4194304 | tf_op jit(solution)/shard_map/sub | solution.py:30
  (4 shorter events, 0.0 us)
Async XLA Ops:
  6.5 18.9 %all-to-all-start = ((bf16[8,192,128]{2,1,0:T(8,128)(2,1)}), bf16[8,192,128]{2,1,0:T(8,128)(2,1)S(1)}, u32[]{:S(2)}, u32[]{:S(2)}) async-start(bf16[8,192,128]{2,1,0:T(8,128)(2,1)} %param.5), calls=%async_computation | async-start | bytes 786432 | tf_op jit(solution)/shard_map/all_to_all | solution.py:13
  25.4 8.6 %copy-start = (s32[32]{0:T(128)S(1)}, s32[32]{0:T(128)}, u32[]{:S(2)}) copy-start(s32[32]{0:T(128)} %param.8) | copy-start | bytes 388
  30.4 17.0 %all-to-all-start.1 = ((bf16[32,48,128]{2,1,0:T(8,128)(2,1)}), bf16[32,48,128]{2,1,0:T(8,128)(2,1)S(1)}, u32[]{:S(2)}, u32[]{:S(2)}) async-start(bf16[32,48,128]{2,1,0:T(8,128)(2,1)} %bitcast.4), calls=%async_computation.1 | async-start | bytes 786432 | tf_op jit(solution)/shard_map/all_to_all | solution.py:19
  33.9 58.6 %all-gather.3.cloned.1.call-start = ((), (), s32[]{:S(2)}) async-start(), calls=%async_computation.3 | async-start | bytes 1966080 | tf_op jit(solution)/shard_map/all_gather | solution.py:23
  63.9 68.5 %all-gather.5.cloned.1.call-start = ((), (), s32[]{:S(2)}) async-start(), calls=%async_computation.4 | async-start | bytes 3538944 | tf_op jit(solution)/shard_map/all_gather | solution.py:26
Sparse Core Ops, SparseCore 0:
  64.0 28.4 all-gather.2
  94.1 38.2 all-gather.4
where the time goes:
time: 148 us
  waiting for transfers between devices  91.7 us (62%)
  blocking collectives  15.8 us (11%)
  between operations  14.1 us (10%)
  starting transfers between devices  9.97 us (7%)
  matrix products  9.54 us (6%)
  local copies, waits for them, and re-layouts  6.37 us (4%)
    all_gather x1, waiting for transfers between devices, body(): lax.all_gather(held, 'col', axis=0, tiled=True)  39.9 us
    all_gather x1, waiting for transfers between devices, body(): column_set = lax.all_gather(held, 'row', axis=0, tiled=True)  25.9 us
    all_to_all x1, blocking collectives, body(): lax.all_to_all(moved, ('row', 'col'), split_axis=0, concat_axis=0, tiled=...  15.8 us
    all_to_all x1, waiting for transfers between devices, body(): lax.all_to_all(pieces, ('row', 'col'), split_axis=0, concat_axis=0, tiled...  13.3 us
    all_to_all x1, waiting for transfers between devices, body(): lax.all_to_all(panel_right, 'col', split_axis=0, concat_axis=1, tiled=True)  11.9 us
    all_to_all x1, starting transfers between devices, body(): lax.all_to_all(panel_right, 'col', split_axis=0, concat_axis=1, tiled=True)  6.35 us
    dot_general x1, matrix products, body(): jnp.einsum('aik,bil->abkl', lax.all_gather(held, 'col', axis=0, tiled=Tru...  5.51 us
    dot_general x1, matrix products, body(): jnp.einsum('ij,bjk->bik', factor_inverse, whole, preferred_element_type=j...  4.03 us
  transfers between devices with their start and end apart: 4, of which 4 were waited for; matrix products, arithmetic and copies ran while one was open for 1% of the time, Pallas kernels for 0%

commit v1 on v0

v1 whole, which is shorter than its diff:
```python
import functools

import jax
import jax.numpy as jnp
from jax import lax
from jax.experimental import pallas as pl
from jax.experimental.pallas import tpu as pltpu
from jax.sharding import PartitionSpec as P

VMEM = pl.BlockSpec(memory_space=pltpu.VMEM)
SMEM = pl.BlockSpec(memory_space=pltpu.SMEM)
ANY = pl.BlockSpec(memory_space=pl.ANY)


def room(mebibytes):
    return pltpu.CompilerParams(vmem_limit_bytes=mebibytes << 20)


def near(value):
    return pltpu.with_memory_space_constraint(value, pltpu.VMEM)


def swap(value, axis, mask):
    count = lax.axis_size(axis)
    return lax.ppermute(value, axis, [(i, i ^ mask) for i in range(count)])


def hypercube(value, axis, count, stride):
    held = [value] + [None] * (count - 1)
    for q in sorted(range(1, count), key=lambda n: (bin(n).count("1"), -n)):
        low = q & -q
        held[q] = swap(held[q ^ low], axis, low * stride)
    return held


def split_kernel(count, place_ref, rank_ref, x_ref, *outs):
    row, blocks = place_ref[0], x_ref.shape[0]
    rank = jnp.full(outs[0].shape[1:], rank_ref[0], jnp.float32).astype(x_ref.dtype)
    for m in range(count):
        outs[m][:blocks] = x_ref[:, row ^ m]
        outs[m][blocks] = rank


def split_rows(place, ranks, x):
    blocks, count, piece, width = x.shape
    return pl.pallas_call(
        functools.partial(split_kernel, count),
        out_shape=[pltpu.VMEM((blocks + 1, piece, width), x.dtype)] * count,
        in_specs=[SMEM, SMEM, VMEM],
        out_specs=[VMEM] * count,
        compiler_params=room(8),
    )(place, ranks, near(x))


def reorder_kernel(n_row, n_col, place_ref, map_ref, *refs):
    pieces, row_outs = refs[:n_row], refs[n_row : 2 * n_row]
    col_outs, rank_out, held = refs[2 * n_row : -2], refs[-2], refs[-1]
    row, col = place_ref[0], place_ref[1]
    rank_out[...] = jnp.zeros_like(rank_out)
    for m in range(n_row):
        held[m * n_col : (m + 1) * n_col] = pieces[m][:n_col]
        rank_out[0, m : m + 1] = pieces[m][n_col, m : m + 1]

    def block(grid_index):
        owner = map_ref[grid_index]
        return held[((owner // n_col) ^ row) * n_col + owner % n_col]

    for m in range(n_row):
        for a in range(n_col):
            row_outs[m][a] = block((row ^ m) * n_col + a)
    for q in range(n_col // 2):
        for j in range(2):
            for b in range(n_row):
                col_outs[q][j, b] = block(b * n_col + (col ^ (2 * q + j)))


def reorder(place, owner_map, pieces, n_row, n_col):
    _, piece, width = pieces[0].shape
    dtype = pieces[0].dtype
    outs = pl.pallas_call(
        functools.partial(reorder_kernel, n_row, n_col),
        out_shape=[pltpu.VMEM((n_col, piece, width), dtype)] * n_row
        + [pltpu.VMEM((2, n_row, piece, width), dtype)] * (n_col // 2)
        + [pltpu.VMEM((1, piece, width), dtype)],
        in_specs=[SMEM, SMEM] + [VMEM] * n_row,
        out_specs=[VMEM] * (n_row + n_col // 2 + 1),
        scratch_shapes=[pltpu.VMEM((n_row * n_col, piece, width), dtype)],
        compiler_params=room(8),
    )(place, owner_map, *map(near, pieces))
    return outs[:n_row], outs[n_row:-1], outs[-1]


def solve_kernel(n_row, n_col, piece, step, place_ref, factor_ref, turned_ref, *refs):
    parts, out, whole = refs[:-2], refs[-2], refs[-1]
    row, col = place_ref[0], place_ref[1]
    width = parts[0].shape[-1]
    order = factor_ref.shape[0]
    if len(parts) == 1:
        whole[...] = parts[0][...]
    else:
        for m in range(n_row):
            for j in range(2):
                for q in range(n_col // 2):
                    start = ((col ^ (2 * q + j)) * n_row + (row ^ m)) * piece
                    rows = pl.ds(pl.multiple_of(start, piece), piece)
                    for b in range(n_row):
                        whole[rows, b * width : (b + 1) * width] = parts[m][j, q, b]
    for top in reversed(range(0, order, step)):
        end = top + step
        left = jnp.dot(factor_ref[top:end, :end], whole[:end], preferred_element_type=jnp.float32)
        whole[top:end] = left.astype(whole.dtype)
    for top in range(0, order, step):
        end = top + step
        both = jnp.dot(turned_ref[top:end, top:], whole[top:], preferred_element_type=jnp.float32)
        out[top:end] = both.astype(out.dtype)


def solve(place, factor, turned, parts, n_row, n_col, piece):
    order, width = factor.shape[0], parts[0].shape[-1]
    step = 256 if order % 256 == 0 else order
    if piece % 16:
        stacked = jnp.stack(parts).reshape(n_row, n_col, n_row, piece, width)
        col, row = jnp.arange(n_col)[:, None] ^ place[1], jnp.arange(n_row)[None] ^ place[0]
        parts = stacked[row, (col % 2) * (n_col // 2) + col // 2]
        parts = [parts.transpose(0, 1, 3, 2, 4).reshape(order, n_row * width)]
    return pl.pallas_call(
        functools.partial(solve_kernel, n_row, n_col, piece, step),
        out_shape=pltpu.VMEM((order, n_row * width), factor.dtype),
        in_specs=[SMEM, VMEM, VMEM] + [VMEM] * len(parts),
        out_specs=VMEM,
        scratch_shapes=[pltpu.VMEM((order, n_row * width), factor.dtype)],
        compiler_params=room(24),
    )(place, factor, turned, *map(near, parts))


def strip(ref, a, n_row, n_col):
    if ref.shape[0] == n_col:
        return ref[a]
    return jnp.concatenate([ref[n * n_col + a] for n in range(n_row)], axis=0)


def gram_of(n_row, n_col, a, strips, turned):
    left = jnp.concatenate([strip(ref, a, n_row, n_col) for ref in strips], axis=0)
    return lax.dot_general(
        left, turned[...], (((0,), (0,)), ((), ())), preferred_element_type=jnp.float32
    )


def turn_rows(n_row, n_col, piece, masks, place_ref, both_ref, turned):
    if piece % 16:
        turned[...] = both_ref[...]
        return
    row, col = place_ref[0], place_ref[1]
    for i, m in enumerate(masks):
        for n in range(n_row):
            start = ((col ^ m) * n_row + (row ^ n)) * piece
            rows = pl.ds(pl.multiple_of(start, piece), piece)
            there = (i * n_row + n) * piece
            turned[there : there + piece] = both_ref[rows]


def gram_first_kernel(n_row, n_col, piece, masks, place_ref, both_ref, *refs):
    strips, out, turned = refs[:-2], refs[-2], refs[-1]
    turn_rows(n_row, n_col, piece, masks, place_ref, both_ref, turned)
    for a in range(n_col):
        out[a] = gram_of(n_row, n_col, a, strips, turned)


def gram_last_kernel(n_row, n_col, piece, masks, place_ref, map_ref, both_ref, first_ref, cores_ref, *refs):
    strips, chunks = refs[: len(masks)], refs[len(masks) : len(masks) + n_col]
    out, turned, table = refs[-3:]
    row, col = place_ref[0], place_ref[1]
    width = cores_ref.shape[-1]
    turn_rows(n_row, n_col, piece, masks, place_ref, both_ref, turned)
    for m in range(n_col):
        for n in range(n_row):
            rank = chunks[m][n_row * n_col, n : n + 1].astype(jnp.float32)
            table[m * n_row + n] = jnp.broadcast_to(rank, table.shape[1:])
    down = lax.broadcasted_iota(jnp.int32, (width, width), 0).astype(jnp.float32)
    across = lax.broadcasted_iota(jnp.int32, (width, width), 1).astype(jnp.float32)

    def rank_of(grid_index):
        owner = map_ref[grid_index]
        entry = ((owner % n_col) ^ col) * n_row + ((owner // n_col) ^ row)
        return table[entry][:1]

    for a in range(n_col):
        gram = gram_of(n_row, n_col, a, strips, turned) + first_ref[a]
        deep = down < rank_of(row * n_col + a)
        for b in range(n_row):
            keep = deep & (across < rank_of(b * n_col + col))
            tile = gram[:, b * width : (b + 1) * width]
            out[a, b] = cores_ref[a, b] - jnp.where(keep, tile, 0.0)


def gram_update(place, owner_map, both, cores, chunks, n_row, n_col, piece):
    order, total = both.shape
    width = cores.shape[-1]
    strips = chunks
    whole = both.reshape(n_col, n_row, piece, total)
    if piece % 16:
        strips = [
            chunk[:-1].reshape(n_row, n_col, piece, width).transpose(1, 0, 2, 3).reshape(n_col, -1, width)
            for chunk in chunks
        ]

    def rows_for(masks):
        if piece % 16 == 0:
            return both
        there = jnp.asarray(masks)[:, None] ^ place[1], jnp.arange(n_row)[None] ^ place[0]
        return whole[there].reshape(-1, total)

    cut = n_col - 2
    height = order // n_col
    first = pl.pallas_call(
        functools.partial(gram_first_kernel, n_row, n_col, piece, tuple(range(cut))),
        out_shape=pltpu.VMEM((n_col, width, total), jnp.float32),
        in_specs=[SMEM, VMEM] + [VMEM] * cut,
        out_specs=VMEM,
        scratch_shapes=[pltpu.VMEM((cut * height, total), both.dtype)],
        compiler_params=room(16),
    )(place, near(rows_for(range(cut))), *map(near, strips[:cut]))
    return pl.pallas_call(
        functools.partial(gram_last_kernel, n_row, n_col, piece, tuple(range(cut, n_col))),
        out_shape=jax.ShapeDtypeStruct(cores.shape, cores.dtype),
        in_specs=[SMEM, SMEM] + [VMEM] * (3 + n_col - cut + n_col),
        out_specs=VMEM,
        scratch_shapes=[
            pltpu.VMEM(((n_col - cut) * height, total), both.dtype),
            pltpu.VMEM((n_row * n_col, 8, width), jnp.float32),
        ],
        compiler_params=room(24),
    )(place, owner_map, near(rows_for(range(cut, n_col))), near(first), cores, *map(near, strips[cut:]), *map(near, chunks))


def body(panel_right, factor_inverse, ranks, owner_map, cores):
    n_row = lax.axis_size("row")
    n_col = lax.axis_size("col")
    blocks, rows, width = panel_right.shape
    piece = rows // n_row
    row = lax.axis_index("row")
    col = lax.axis_index("col")
    place = jnp.stack([row, col]).astype(jnp.int32)
    planes = n_col // 2

    parts = split_rows(place, ranks, panel_right.reshape(blocks, n_row, piece, width))
    parts = [parts[0]] + [swap(parts[m], "row", m) for m in range(1, n_row)]
    row_parts, col_parts, rank_rows = reorder(place, owner_map, parts, n_row, n_col)

    col_parts = [col_parts[0]] + [swap(col_parts[q], "col", 2 * q) for q in range(1, planes)]
    row_parts = [row_parts[0]] + [swap(row_parts[m], "row", m) for m in range(1, n_row)]
    mine = jnp.stack([part[0] for part in col_parts])
    theirs = swap(jnp.stack([part[1] for part in col_parts]), "col", 1)
    col_set = hypercube(jnp.stack([mine, theirs]), "row", n_row, 1)
    row_set = hypercube(jnp.concatenate(row_parts + [rank_rows]), "col", planes, 2)
    chunks = []
    for part in row_set:
        chunks += [part, swap(part, "col", 1)]

    turned = lax.optimization_barrier(factor_inverse.T)
    both = solve(place, factor_inverse, turned, col_set, n_row, n_col, piece)
    return gram_update(place, owner_map, both, cores[0, 0], chunks, n_row, n_col, piece)[None, None]


def solution(mesh):
    return jax.shard_map(
        body,
        mesh=mesh,
        in_specs=(
            P("row", "col", None),
            P(),
            P(("row", "col")),
            P(),
            P("row", "col", None, None, None, None),
        ),
        out_specs=P("row", "col", None, None, None, None),
        check_vma=False,
    )
```

time: 148 us -> 87.9 us (0.59)
  waiting for transfers between devices: 91.7 us -> 39.1 us
  blocking collectives: 15.8 us -> 0 us
  between operations: 14.1 us -> 0.85 us
  Pallas kernels: 0 us -> 10.9 us
  local copies, waits for them, and re-layouts: 6.37 us -> 16.6 us
  starting transfers between devices: 9.97 us -> 19.8 us
  matrix products: 9.54 us -> 0 us
    all_gather x2 -> x0, waiting for transfers between devices: 65.8 us -> none  [the longest x1 39.9 us: body(): lax.all_gather(held, 'col', axis=0, tiled=True)]
    ppermute x0 -> x20, waiting for transfers between devices: none -> 39.1 us  [swap(): return lax.ppermute(value, axis, [(i, i ^ mask) for i in range(count)])]
    all_to_all x2 -> x0, waiting for transfers between devices: 25.2 us -> none  [the longest x1 13.3 us: body(): lax.all_to_all(pieces, ('row', 'col'), split_axis=0, concat_axis=0, tiled...]
    ppermute x0 -> x20, starting transfers between devices: none -> 19.8 us  [swap(): return lax.ppermute(value, axis, [(i, i ^ mask) for i in range(count)])]
    all_to_all x1 -> x0, blocking collectives: 15.8 us -> none  [body(): lax.all_to_all(moved, ('row', 'col'), split_axis=0, concat_axis=0, tiled=...]
    unnamed x3 -> x25, local copies, waits for them, and re-layouts: 1.94 us -> 16.5 us
    pallas_call x0 -> x5, Pallas kernels: none -> 10.9 us  [the longest x1 4.55 us: solve(): pl.pallas_call(functools.partial(solve_kernel, n_row, n_col, piece, step)...]
    all_to_all x2 -> x0, starting transfers between devices: 9.89 us -> none  [the longest x1 6.35 us: body(): lax.all_to_all(panel_right, 'col', split_axis=0, concat_axis=1, tiled=True)]
  transfers between devices with their start and end apart: 4 -> 20, of which waited for: 4 -> 11; matrix products, arithmetic and copies ran while one was open for 1% -> 8% of each run, Pallas kernels for 0% -> 8%
where the time goes in v1:
time: 87.9 us; the launch traced here: 87.4 us
  waiting for transfers between devices  39.1 us (44%)
  starting transfers between devices  19.8 us (23%)
  local copies, waits for them, and re-layouts  16.6 us (19%)
  Pallas kernels  10.9 us (12%)
    ppermute x20, waiting for transfers between devices, swap(): return lax.ppermute(value, axis, [(i, i ^ mask) for i in range(count)])  39.1 us
    ppermute x20, starting transfers between devices, swap(): return lax.ppermute(value, axis, [(i, i ^ mask) for i in range(count)])  19.8 us
    unnamed x25, local copies, waits for them, and re-layouts  16.5 us
    pallas_call x1, Pallas kernels, solve(): pl.pallas_call(functools.partial(solve_kernel, n_row, n_col, piece, step)...  4.55 us
    pallas_call x1, Pallas kernels, gram_update(): pl.pallas_call(functools.partial(gram_last_kernel, n_row, n_col, piece, t...  2.65 us
    pallas_call x1, Pallas kernels, gram_update(): pl.pallas_call(functools.partial(gram_first_kernel, n_row, n_col, piece,...  2.15 us
  transfers between devices with their start and end apart: 20, of which 11 were waited for; matrix products, arithmetic and copies ran while one was open for 8% of the time, Pallas kernels for 8%

profile of v1, /device:TPU:0, one launch (start us, length us, event | category | flops | bytes accessed | tf_op | source)
XLA Modules:
  0.0 87.4 jit_solution(12247771268034182193)
XLA Ops:
  0.7 0.1 pad_add_fusion.place_ref
  0.7 0.0 copy-start.7
  0.7 1.0 %copy-done.7 = bf16[8,192,128]{2,1,0:T(8,128)(2,1)S(1)} copy-done((bf16[8,192,128]{2,1,0:T(8,128)(2,1)S(1)}, bf16[8,192,128]{2,1,0:T(8,128)(2,1)}, u32[]{:S(2)}) %copy-start.7) | copy-done | bytes 393240
  1.7 0.6 shard_map.55
  2.3 3.0 %collective-permute-start = (bf16[9,48,128]{2,1,0:T(8,128)(2,1)S(1)}, bf16[9,48,128]{2,1,0:T(8,128)(2,1)S(1)}, u32[]{:S(2)}, u32[]{:S(2)}) collective-permute-start(bf16[9,48,128]{2,1,0:T(8,128)(2,1)S(1)} %get-tuple-element.19), channel_id=1, source_target_pairs={{0,8},{8,0},{16,24},{24,16},{1,9},{9,1},{17,25},{25,17},{2,10},{10... | collective-permute-start | bytes 331784 | tf_op jit(solution)/shard_map/ppermute | solution.py:25
  5.3 1.5 %collective-permute-start.1 = (bf16[9,48,128]{2,1,0:T(8,128)(2,1)S(1)}, bf16[9,48,128]{2,1,0:T(8,128)(2,1)S(1)}, u32[]{:S(2)}, u32[]{:S(2)}) collective-permute-start(bf16[9,48,128]{2,1,0:T(8,128)(2,1)S(1)} %get-tuple-element.20), channel_id=1, source_target_pairs={{0,16},{8,24},{16,0},{24,8},{1,17},{9,25},{17,1},{25,9},{2,18},{10... | collective-permute-start | bytes 331784 | tf_op jit(solution)/shard_map/ppermute | solution.py:25
  6.9 0.0 collective-permute-start.2
  6.9 1.9 %collective-permute-done.refs_1_ = bf16[9,48,128]{2,1,0:T(8,128)(2,1)S(1)} collective-permute-done((bf16[9,48,128]{2,1,0:T(8,128)(2,1)S(1)}, bf16[9,48,128]{2,1,0:T(8,128)(2,1)S(1)}, u32[]{:S(2)}, u32[]{:S(2)}) %collective-permute-start) | collective-permute-done | bytes 110624 | tf_op jit(solution)/shard_map/ppermute | solution.py:25
  8.8 2.5 %collective-permute-done.1.refs_2_ = bf16[9,48,128]{2,1,0:T(8,128)(2,1)S(1)} collective-permute-done((bf16[9,48,128]{2,1,0:T(8,128)(2,1)S(1)}, bf16[9,48,128]{2,1,0:T(8,128)(2,1)S(1)}, u32[]{:S(2)}, u32[]{:S(2)}) %collective-permute-start.1) | collective-permute-done | bytes 110624 | tf_op jit(solution)/shard_map/ppermute | solution.py:25
  11.3 1.2 %collective-permute-done.2.refs_3_ = bf16[9,48,128]{2,1,0:T(8,128)(2,1)S(1)} collective-permute-done((bf16[9,48,128]{2,1,0:T(8,128)(2,1)S(1)}, bf16[9,48,128]{2,1,0:T(8,128)(2,1)S(1)}, u32[]{:S(2)}, u32[]{:S(2)}) %collective-permute-start.2) | collective-permute-done | bytes 110624 | tf_op jit(solution)/shard_map/ppermute | solution.py:25
  12.5 0.0 copy-start.8
  12.5 0.7 copy-done.8
  13.2 1.0 %shard_map.56 = (bf16[8,48,128]{2,1,0:T(8,128)(2,1)S(1)}, bf16[8,48,128]{2,1,0:T(8,128)(2,1)S(1)}, bf16[8,48,128]{2,1,0:T(8,128)(2,1)S(1)}, bf16[8,48,128]{2,1,0...) custom-call(s32[2]{0:T(128)S(1)} %pad_add_fusion.place_ref, ...), custom_call_target="tpu_custom_call" | custom-call | tf_op jit(solution)/shard_map/pallas_call | solution.py:80
  14.2 3.7 %collective-permute-start.5 = (bf16[2,4,48,128]{3,2,1,0:T(8,128)(2,1)S(1)}, bf16[2,4,48,128]{3,2,1,0:T(8,128)(2,1)S(1)}, u32[]{:S(2)}, u32[]{:S(2)}) collective-permute-start(bf16[2,4,48,128]{3,2,1,0:T(8,128)(2,1)S(1)} %get-tuple-element.25), channel_id=1, source_target_pairs={{0,6},{1,7},{2,4},{3,5},{4,2},{5,3},{6,0},{7,1},{8,14},{9,15},{10,... | collective-permute-start | bytes 294920 | tf_op jit(solution)/shard_map/ppermute | solution.py:25
  17.8 0.0 collective-permute-start.4
  17.8 0.8 collective-permute-start.3
  18.6 1.0 %collective-permute-start.10 = (bf16[8,48,128]{2,1,0:T(8,128)(2,1)S(1)}, bf16[8,48,128]{2,1,0:T(8,128)(2,1)S(1)}, u32[]{:S(2)}, u32[]{:S(2)}) collective-permute-start(bf16[8,48,128]{2,1,0:T(8,128)(2,1)S(1)} %get-tuple-element.27), channel_id=1, source_target_pairs={{0,8},{8,0},{16,24},{24,16},{1,9},{9,1},{17,25},{25,17},{2,10},{10... | collective-permute-start | bytes 294920 | tf_op jit(solution)/shard_map/ppermute | solution.py:25
  19.6 0.8 collective-permute-start.11
  20.5 3.4 %collective-permute-done.10 = bf16[8,48,128]{2,1,0:T(8,128)(2,1)S(1)} collective-permute-done((bf16[8,48,128]{2,1,0:T(8,128)(2,1)S(1)}, bf16[8,48,128]{2,1,0:T(8,128)(2,1)S(1)}, u32[]{:S(2)}, u32[]{:S(2)}) %collective-permute-start.10) | collective-permute-done | bytes 98336 | tf_op jit(solution)/shard_map/ppermute | solution.py:25
  23.9 0.7 collective-permute-start.12
  24.5 0.8 collective-permute-done.11
  25.3 4.1 %collective-permute-done.12 = bf16[8,48,128]{2,1,0:T(8,128)(2,1)S(1)} collective-permute-done((bf16[8,48,128]{2,1,0:T(8,128)(2,1)S(1)}, bf16[8,48,128]{2,1,0:T(8,128)(2,1)S(1)}, u32[]{:S(2)}, u32[]{:S(2)}) %collective-permute-start.12) | collective-permute-done | bytes 98336 | tf_op jit(solution)/shard_map/ppermute | solution.py:25
  29.4 2.1 %collective-permute-start.16 = (bf16[33,48,128]{2,1,0:T(8,128)(2,1)S(1)}, bf16[33,48,128]{2,1,0:T(8,128)(2,1)S(1)}, u32[]{:S(2)}, u32[]{:S(2)}) collective-permute-start(bf16[33,48,128]{2,1,0:T(8,128)(2,1)S(1)} %constant_dynamic-update-slice_fusion.refs_0_.refs_2_), channel_id=1, source_target_pairs={{0,4},{1,5},{2,6},{3,7},{4,0},{5,1},{6,2},{7,3},{8,12},{9,13},{10,... | collective-permute-start | bytes 1216520 | tf_op jit(solution)/shard_map/ppermute | solution.py:25
  31.5 0.0 collective-permute-done.5
  31.5 0.0 collective-permute-done.4
  31.5 0.0 collective-permute-done.3
  31.6 0.1 collective-permute-start.6
  31.7 2.4 %collective-permute-start.14 = (bf16[33,48,128]{2,1,0:T(8,128)(2,1)S(1)}, bf16[33,48,128]{2,1,0:T(8,128)(2,1)S(1)}, u32[]{:S(2)}, u32[]{:S(2)}) collective-permute-start(bf16[33,48,128]{2,1,0:T(8,128)(2,1)S(1)} %constant_dynamic-update-slice_fusion.refs_0_.refs_2_), channel_id=1, source_target_pairs={{0,2},{1,3},{2,0},{3,1},{4,6},{5,7},{6,4},{7,5},{8,10},{9,11},{10,... | collective-permute-start | bytes 1216520 | tf_op jit(solution)/shard_map/ppermute | solution.py:25
  34.1 12.0 %collective-permute-done.16.refs_4_.refs_6_ = bf16[33,48,128]{2,1,0:T(8,128)(2,1)S(1)} collective-permute-done((bf16[33,48,128]{2,1,0:T(8,128)(2,1)S(1)}, bf16[33,48,128]{2,1,0:T(8,128)(2,1)S(1)}, u32[]{:S(2)}, u32[]{:S(2)}) %collective-permute-start.16) | collective-permute-done | bytes 405536 | tf_op jit(solution)/shard_map/ppermute | solution.py:25
  46.0 0.2 collective-permute-start.18
  46.2 0.0 collective-permute-done.6
  46.2 1.5 %collective-permute-start.7 = (bf16[2,4,4,48,128]{4,3,2,1,0:T(8,128)(2,1)S(1)}, bf16[2,4,4,48,128]{4,3,2,1,0:T(8,128)(2,1)S(1)}, u32[]{:S(2)}, u32[]{:S(2)}) collective-permute-start(bf16[2,4,4,48,128]{4,3,2,1,0:T(8,128)(2,1)S(1)} %pad_maximum_fusion.refs_0_), channel_id=1, source_target_pairs={{0,8},{8,0},{16,24},{24,16},{1,9},{9,1},{17,25},{25,17},{2,10},{10... | collective-permute-start | bytes 1179656 | tf_op jit(solution)/shard_map/ppermute | solution.py:25
  47.8 0.6 collective-permute-start.8
  48.4 0.0 copy-start.3
  48.4 0.7 copy-done.3
  49.1 0.0 collective-permute-start.13
  49.1 1.7 %collective-permute-done.14.refs_2_.refs_4_ = bf16[33,48,128]{2,1,0:T(8,128)(2,1)S(1)} collective-permute-done((bf16[33,48,128]{2,1,0:T(8,128)(2,1)S(1)}, bf16[33,48,128]{2,1,0:T(8,128)(2,1)S(1)}, u32[]{:S(2)}, u32[]{:S(2)}) %collective-permute-start.14) | collective-permute-done | bytes 405536 | tf_op jit(solution)/shard_map/ppermute | solution.py:25
  50.9 0.0 collective-permute-start.15
  50.9 5.9 %collective-permute-done.7.refs_1_ = bf16[2,4,4,48,128]{4,3,2,1,0:T(8,128)(2,1)S(1)} collective-permute-done((bf16[2,4,4,48,128]{4,3,2,1,0:T(8,128)(2,1)S(1)}, bf16[2,4,4,48,128]{4,3,2,1,0:T(8,128)(2,1)S(1)}, u32[]{:S(2)}, u32[]{:S(2)}) %collective-permute-start.7) | collective-permute-done | bytes 393248 | tf_op jit(solution)/shard_map/ppermute | solution.py:25
  56.8 0.0 copy-start.5
  56.8 0.7 copy-done.5
  57.5 0.0 collective-permute-start.17
  57.5 1.9 %collective-permute-done.18.refs_0_.refs_8_ = bf16[33,48,128]{2,1,0:T(8,128)(2,1)S(1)} collective-permute-done((bf16[33,48,128]{2,1,0:T(8,128)(2,1)S(1)}, bf16[33,48,128]{2,1,0:T(8,128)(2,1)S(1)}, u32[]{:S(2)}, u32[]{:S(2)}) %collective-permute-start.18) | collective-permute-done | bytes 405536 | tf_op jit(solution)/shard_map/ppermute | solution.py:25
  59.4 0.0 collective-permute-start.19
  59.4 0.0 collective-permute-done.8.refs_2_
  59.4 1.5 %collective-permute-start.9 = (bf16[2,4,4,48,128]{4,3,2,1,0:T(8,128)(2,1)}, bf16[2,4,4,48,128]{4,3,2,1,0:T(8,128)(2,1)}, u32[]{:S(2)}, u32[]{:S(2)}) collective-permute-start(bf16[2,4,4,48,128]{4,3,2,1,0:T(8,128)(2,1)} %collective-permute-done.8.refs_2_), channel_id=1, source_target_pairs={{0,8},{8,0},{16,24},{24,16},{1,9},{9,1},{17,25},{25,17},{2,10},{10... | collective-permute-start | bytes 1179656 | tf_op jit(solution)/shard_map/ppermute | solution.py:25
  60.9 6.6 %copy.6 = bf16[1536,1536]{0,1:T(8,128)(2,1)} copy(bf16[1536,1536]{1,0:T(8,128)(2,1)} %factor_ref.1) | data formatting | bytes 9437184 | tf_op args[1]
  67.5 3.7 %collective-permute-done.9.refs_3_ = bf16[2,4,4,48,128]{4,3,2,1,0:T(8,128)(2,1)} collective-permute-done((bf16[2,4,4,48,128]{4,3,2,1,0:T(8,128)(2,1)}, bf16[2,4,4,48,128]{4,3,2,1,0:T(8,128)(2,1)}, u32[]{:S(2)}, u32[]{:S(2)}) %collective-permute-start.9) | collective-permute-done | bytes 393248 | tf_op jit(solution)/shard_map/ppermute | solution.py:25
  71.3 0.0 copy-start
  71.3 2.3 %copy-done = bf16[1536,1536]{1,0:T(8,128)(2,1)S(1)} copy-done((bf16[1536,1536]{1,0:T(8,128)(2,1)S(1)}, bf16[1536,1536]{1,0:T(8,128)(2,1)}, u32[]{:S(2)}) %copy-start) | copy-done | bytes 4718616
  73.6 2.3 %copy-done.1 = bf16[1536,1536]{0,1:T(8,128)(2,1)S(1)} copy-done((bf16[1536,1536]{0,1:T(8,128)(2,1)S(1)}, bf16[1536,1536]{0,1:T(8,128)(2,1)}, u32[]{:S(2)}) %copy-start.1) | copy-done | bytes 4718616
  75.9 1.0 %copy-done.4 = bf16[2,4,4,48,128]{4,3,2,1,0:T(8,128)(2,1)S(1)} copy-done((bf16[2,4,4,48,128]{4,3,2,1,0:T(8,128)(2,1)S(1)}, bf16[2,4,4,48,128]{4,3,2,1,0:T(8,128)(2,1)}, u32[]{:S(2)}) %copy-start.4) | copy-done | bytes 393240
  76.9 1.0 %copy-done.6 = bf16[2,4,4,48,128]{4,3,2,1,0:T(8,128)(2,1)S(1)} copy-done((bf16[2,4,4,48,128]{4,3,2,1,0:T(8,128)(2,1)S(1)}, bf16[2,4,4,48,128]{4,3,2,1,0:T(8,128)(2,1)}, u32[]{:S(2)}) %copy-start.6) | copy-done | bytes 393240
  77.9 4.5 %shard_map.57.both_ref = bf16[1536,512]{1,0:T(8,128)(2,1)S(1)} custom-call(s32[2]{0:T(128)S(1)} %pad_add_fusion.place_ref, bf16[1536,1536]{1,0:T(8,128)(2,1)S(1)} %copy-done, bf16[1536,1536]{1,0:T(8,128)(2,1)S(1)} %bitcast.9, bf16[2,4,4,48,128]{4,3,2,1,0:T(8,128)(2,1)S(1)} %copy-done.4, bf16[2,4,4,48,128]{4,3,2,1,0:T(8,128)(2,1)S(1)} %copy-done.6, ...), custom_call_target="tpu_custom_call" | custom-call | tf_op jit(solution)/shard_map/pallas_call | solution.py:126
  82.5 0.0 copy-start.2
  82.5 0.0 copy-start.9
  82.5 0.0 collective-permute-done.13.refs_1_.refs_3_
  82.5 0.0 collective-permute-done.15.refs_3_.refs_5_
  82.5 0.0 collective-permute-done.17.refs_5_.refs_7_
  82.5 2.2 %shard_map.58.first_ref = f32[8,128,512]{2,1,0:T(8,128)S(1)} custom-call(s32[2]{0:T(128)S(1)} %pad_add_fusion.place_ref, bf16[1536,512]{1,0:T(8,128)(2,1)S(1)} %shard_map.57.both_ref, bf16[33,48,128]{2,1,0:T(8,128)(2,1)S(1)} %constant_dynamic-update-slice_fusion.refs_0_.refs_2_, bf16[33,48,128]{2,1,0:T(8,128)(2,1)S(1)} %collective-permute-done.13.refs_1_.refs_3_, ...), custom_call_target="tpu_custom_call" | custom-call | tf_op jit(solution)/shard_map/pallas_call | solution.py:215
  84.7 0.0 collective-permute-done.19.refs_1_.refs_9_
  84.7 0.0 copy-done.2
  84.7 0.0 copy-done.9
  84.7 2.6 %shard_map.59 = f32[8,4,128,128]{3,2,1,0:T(8,128)} custom-call(s32[2]{0:T(128)S(1)} %pad_add_fusion.place_ref, s32[32]{0:T(128)S(1)} %copy-done.9, bf16[1536,512]{1,0:T(8,128)(2,1)S(1)} %shard_map.57.both_ref, f32[8,128,512]{2,1,0:T(8,128)S(1)} %shard_map.58.first_ref, f32[8,4,128,128]{3,2,1,0:T(8,128)S(1)} %bitcast.10, ...), custom_call_target="tpu_custom_call" | custom-call | tf_op jit(solution)/shard_map/pallas_call | solution.py:223
  (15 shorter events, 0.2 us)
Async XLA Ops:
  0.7 1.0 %copy-start.7 = (bf16[8,192,128]{2,1,0:T(8,128)(2,1)S(1)}, bf16[8,192,128]{2,1,0:T(8,128)(2,1)}, u32[]{:S(2)}) copy-start(bf16[8,192,128]{2,1,0:T(8,128)(2,1)} %param.5) | copy-start | bytes 1179652
  2.3 6.5 %collective-permute-start = (bf16[9,48,128]{2,1,0:T(8,128)(2,1)S(1)}, bf16[9,48,128]{2,1,0:T(8,128)(2,1)S(1)}, u32[]{:S(2)}, u32[]{:S(2)}) collective-permute-start(bf16[9,48,128]{2,1,0:T(8,128)(2,1)S(1)} %get-tuple-element.19), channel_id=1, source_target_pairs={{0,8},{8,0},{16,24},{24,16},{1,9},{9,1},{17,25},{25,17},{2,10},{10... | collective-permute-start | bytes 331784 | tf_op jit(solution)/shard_map/ppermute | solution.py:25
  5.3 5.9 %collective-permute-start.1 = (bf16[9,48,128]{2,1,0:T(8,128)(2,1)S(1)}, bf16[9,48,128]{2,1,0:T(8,128)(2,1)S(1)}, u32[]{:S(2)}, u32[]{:S(2)}) collective-permute-start(bf16[9,48,128]{2,1,0:T(8,128)(2,1)S(1)} %get-tuple-element.20), channel_id=1, source_target_pairs={{0,16},{8,24},{16,0},{24,8},{1,17},{9,25},{17,1},{25,9},{2,18},{10... | collective-permute-start | bytes 331784 | tf_op jit(solution)/shard_map/ppermute | solution.py:25
  6.9 5.6 %collective-permute-start.2 = (bf16[9,48,128]{2,1,0:T(8,128)(2,1)S(1)}, bf16[9,48,128]{2,1,0:T(8,128)(2,1)S(1)}, u32[]{:S(2)}, u32[]{:S(2)}) collective-permute-start(bf16[9,48,128]{2,1,0:T(8,128)(2,1)S(1)} %get-tuple-element.21), channel_id=1, source_target_pairs={{0,24},{8,16},{16,8},{24,0},{1,25},{9,17},{17,9},{25,1},{2,26},{10... | collective-permute-start | bytes 331784 | tf_op jit(solution)/shard_map/ppermute | solution.py:25
  12.5 0.7 copy-start.8
  14.2 17.3 %collective-permute-start.5 = (bf16[2,4,48,128]{3,2,1,0:T(8,128)(2,1)S(1)}, bf16[2,4,48,128]{3,2,1,0:T(8,128)(2,1)S(1)}, u32[]{:S(2)}, u32[]{:S(2)}) collective-permute-start(bf16[2,4,48,128]{3,2,1,0:T(8,128)(2,1)S(1)} %get-tuple-element.25), channel_id=1, source_target_pairs={{0,6},{1,7},{2,4},{3,5},{4,2},{5,3},{6,0},{7,1},{8,14},{9,15},{10,... | collective-permute-start | bytes 294920 | tf_op jit(solution)/shard_map/ppermute | solution.py:25
  17.8 13.7 %collective-permute-start.4 = (bf16[2,4,48,128]{3,2,1,0:T(8,128)(2,1)S(1)}, bf16[2,4,48,128]{3,2,1,0:T(8,128)(2,1)S(1)}, u32[]{:S(2)}, u32[]{:S(2)}) collective-permute-start(bf16[2,4,48,128]{3,2,1,0:T(8,128)(2,1)S(1)} %get-tuple-element.24), channel_id=1, source_target_pairs={{0,4},{1,5},{2,6},{3,7},{4,0},{5,1},{6,2},{7,3},{8,12},{9,13},{10,... | collective-permute-start | bytes 294920 | tf_op jit(solution)/shard_map/ppermute | solution.py:25
  17.8 13.7 %collective-permute-start.3 = (bf16[2,4,48,128]{3,2,1,0:T(8,128)(2,1)S(1)}, bf16[2,4,48,128]{3,2,1,0:T(8,128)(2,1)S(1)}, u32[]{:S(2)}, u32[]{:S(2)}) collective-permute-start(bf16[2,4,48,128]{3,2,1,0:T(8,128)(2,1)S(1)} %get-tuple-element.23), channel_id=1, source_target_pairs={{0,2},{1,3},{2,0},{3,1},{4,6},{5,7},{6,4},{7,5},{8,10},{9,11},{10,... | collective-permute-start | bytes 294920 | tf_op jit(solution)/shard_map/ppermute | solution.py:25
  18.6 5.2 %collective-permute-start.10 = (bf16[8,48,128]{2,1,0:T(8,128)(2,1)S(1)}, bf16[8,48,128]{2,1,0:T(8,128)(2,1)S(1)}, u32[]{:S(2)}, u32[]{:S(2)}) collective-permute-start(bf16[8,48,128]{2,1,0:T(8,128)(2,1)S(1)} %get-tuple-element.27), channel_id=1, source_target_pairs={{0,8},{8,0},{16,24},{24,16},{1,9},{9,1},{17,25},{25,17},{2,10},{10... | collective-permute-start | bytes 294920 | tf_op jit(solution)/shard_map/ppermute | solution.py:25
  19.6 5.7 %collective-permute-start.11 = (bf16[8,48,128]{2,1,0:T(8,128)(2,1)S(1)}, bf16[8,48,128]{2,1,0:T(8,128)(2,1)S(1)}, u32[]{:S(2)}, u32[]{:S(2)}) collective-permute-start(bf16[8,48,128]{2,1,0:T(8,128)(2,1)S(1)} %get-tuple-element.28), channel_id=1, source_target_pairs={{0,16},{8,24},{16,0},{24,8},{1,17},{9,25},{17,1},{25,9},{2,18},{10... | collective-permute-start | bytes 294920 | tf_op jit(solution)/shard_map/ppermute | solution.py:25
  23.9 5.5 %collective-permute-start.12 = (bf16[8,48,128]{2,1,0:T(8,128)(2,1)S(1)}, bf16[8,48,128]{2,1,0:T(8,128)(2,1)S(1)}, u32[]{:S(2)}, u32[]{:S(2)}) collective-permute-start(bf16[8,48,128]{2,1,0:T(8,128)(2,1)S(1)} %get-tuple-element.29), channel_id=1, source_target_pairs={{0,24},{8,16},{16,8},{24,0},{1,25},{9,17},{17,9},{25,1},{2,26},{10... | collective-permute-start | bytes 294920 | tf_op jit(solution)/shard_map/ppermute | solution.py:25
  29.4 16.6 %collective-permute-start.16 = (bf16[33,48,128]{2,1,0:T(8,128)(2,1)S(1)}, bf16[33,48,128]{2,1,0:T(8,128)(2,1)S(1)}, u32[]{:S(2)}, u32[]{:S(2)}) collective-permute-start(bf16[33,48,128]{2,1,0:T(8,128)(2,1)S(1)} %constant_dynamic-update-slice_fusion.refs_0_.refs_2_), channel_id=1, source_target_pairs={{0,4},{1,5},{2,6},{3,7},{4,0},{5,1},{6,2},{7,3},{8,12},{9,13},{10,... | collective-permute-start | bytes 1216520 | tf_op jit(solution)/shard_map/ppermute | solution.py:25
  31.6 14.6 %collective-permute-start.6 = (bf16[4,4,48,128]{3,2,1,0:T(8,128)(2,1)S(1)}, bf16[4,4,48,128]{3,2,1,0:T(8,128)(2,1)S(1)}, u32[]{:S(2)}, u32[]{:S(2)}) collective-permute-start(bf16[4,4,48,128]{3,2,1,0:T(8,128)(2,1)S(1)} %pad_maximum_fusion.1), channel_id=1, source_target_pairs={{0,1},{1,0},{2,3},{3,2},{4,5},{5,4},{6,7},{7,6},{8,9},{9,8},{10,11... | collective-permute-start | bytes 589832 | tf_op jit(solution)/shard_map/ppermute | solution.py:25
  31.7 19.2 %collective-permute-start.14 = (bf16[33,48,128]{2,1,0:T(8,128)(2,1)S(1)}, bf16[33,48,128]{2,1,0:T(8,128)(2,1)S(1)}, u32[]{:S(2)}, u32[]{:S(2)}) collective-permute-start(bf16[33,48,128]{2,1,0:T(8,128)(2,1)S(1)} %constant_dynamic-update-slice_fusion.refs_0_.refs_2_), channel_id=1, source_target_pairs={{0,2},{1,3},{2,0},{3,1},{4,6},{5,7},{6,4},{7,5},{8,10},{9,11},{10,... | collective-permute-start | bytes 1216520 | tf_op jit(solution)/shard_map/ppermute | solution.py:25
  46.0 13.4 %collective-permute-start.18 = (bf16[33,48,128]{2,1,0:T(8,128)(2,1)S(1)}, bf16[33,48,128]{2,1,0:T(8,128)(2,1)S(1)}, u32[]{:S(2)}, u32[]{:S(2)}) collective-permute-start(bf16[33,48,128]{2,1,0:T(8,128)(2,1)S(1)} %collective-permute-done.16.refs_4_.refs_6_), channel_id=1, source_target_pairs={{0,2},{1,3},{2,0},{3,1},{4,6},{5,7},{6,4},{7,5},{8,10},{9,11},{10,... | collective-permute-start | bytes 1216520 | tf_op jit(solution)/shard_map/ppermute | solution.py:25
  46.2 10.5 %collective-permute-start.7 = (bf16[2,4,4,48,128]{4,3,2,1,0:T(8,128)(2,1)S(1)}, bf16[2,4,4,48,128]{4,3,2,1,0:T(8,128)(2,1)S(1)}, u32[]{:S(2)}, u32[]{:S(2)}) collective-permute-start(bf16[2,4,4,48,128]{4,3,2,1,0:T(8,128)(2,1)S(1)} %pad_maximum_fusion.refs_0_), channel_id=1, source_target_pairs={{0,8},{8,0},{16,24},{24,16},{1,9},{9,1},{17,25},{25,17},{2,10},{10... | collective-permute-start | bytes 1179656 | tf_op jit(solution)/shard_map/ppermute | solution.py:25
  47.8 11.7 %collective-permute-start.8 = (bf16[2,4,4,48,128]{4,3,2,1,0:T(8,128)(2,1)S(1)}, bf16[2,4,4,48,128]{4,3,2,1,0:T(8,128)(2,1)}, u32[]{:S(2)}, u32[]{:S(2)}) collective-permute-start(bf16[2,4,4,48,128]{4,3,2,1,0:T(8,128)(2,1)S(1)} %pad_maximum_fusion.refs_0_), channel_id=1, source_target_pairs={{0,16},{8,24},{16,0},{24,8},{1,17},{9,25},{17,1},{25,9},{2,18},{10... | collective-permute-start | bytes 1179656 | tf_op jit(solution)/shard_map/ppermute | solution.py:25
  48.4 0.7 copy-start.3
  49.1 33.4 %collective-permute-start.13 = (bf16[33,48,128]{2,1,0:T(8,128)(2,1)S(1)}, bf16[33,48,128]{2,1,0:T(8,128)(2,1)S(1)}, u32[]{:S(2)}, u32[]{:S(2)}) collective-permute-start(bf16[33,48,128]{2,1,0:T(8,128)(2,1)S(1)} %constant_dynamic-update-slice_fusion.refs_0_.refs_2_), channel_id=1, source_target_pairs={{0,1},{1,0},{2,3},{3,2},{4,5},{5,4},{6,7},{7,6},{8,9},{9,8},{10,11... | collective-permute-start | bytes 1216520 | tf_op jit(solution)/shard_map/ppermute | solution.py:25
  50.9 31.7 %collective-permute-start.15 = (bf16[33,48,128]{2,1,0:T(8,128)(2,1)S(1)}, bf16[33,48,128]{2,1,0:T(8,128)(2,1)S(1)}, u32[]{:S(2)}, u32[]{:S(2)}) collective-permute-start(bf16[33,48,128]{2,1,0:T(8,128)(2,1)S(1)} %collective-permute-done.14.refs_2_.refs_4_), channel_id=1, source_target_pairs={{0,1},{1,0},{2,3},{3,2},{4,5},{5,4},{6,7},{7,6},{8,9},{9,8},{10,11... | collective-permute-start | bytes 1216520 | tf_op jit(solution)/shard_map/ppermute | solution.py:25
  56.8 0.7 copy-start.5
  57.5 25.0 %collective-permute-start.17 = (bf16[33,48,128]{2,1,0:T(8,128)(2,1)S(1)}, bf16[33,48,128]{2,1,0:T(8,128)(2,1)S(1)}, u32[]{:S(2)}, u32[]{:S(2)}) collective-permute-start(bf16[33,48,128]{2,1,0:T(8,128)(2,1)S(1)} %collective-permute-done.16.refs_4_.refs_6_), channel_id=1, source_target_pairs={{0,1},{1,0},{2,3},{3,2},{4,5},{5,4},{6,7},{7,6},{8,9},{9,8},{10,11... | collective-permute-start | bytes 1216520 | tf_op jit(solution)/shard_map/ppermute | solution.py:25
  59.4 25.3 %collective-permute-start.19 = (bf16[33,48,128]{2,1,0:T(8,128)(2,1)S(1)}, bf16[33,48,128]{2,1,0:T(8,128)(2,1)S(1)}, u32[]{:S(2)}, u32[]{:S(2)}) collective-permute-start(bf16[33,48,128]{2,1,0:T(8,128)(2,1)S(1)} %collective-permute-done.18.refs_0_.refs_8_), channel_id=1, source_target_pairs={{0,1},{1,0},{2,3},{3,2},{4,5},{5,4},{6,7},{7,6},{8,9},{9,8},{10,11... | collective-permute-start | bytes 1216520 | tf_op jit(solution)/shard_map/ppermute | solution.py:25
  59.4 11.8 %collective-permute-start.9 = (bf16[2,4,4,48,128]{4,3,2,1,0:T(8,128)(2,1)}, bf16[2,4,4,48,128]{4,3,2,1,0:T(8,128)(2,1)}, u32[]{:S(2)}, u32[]{:S(2)}) collective-permute-start(bf16[2,4,4,48,128]{4,3,2,1,0:T(8,128)(2,1)} %collective-permute-done.8.refs_2_), channel_id=1, source_target_pairs={{0,8},{8,0},{16,24},{24,16},{1,9},{9,1},{17,25},{25,17},{2,10},{10... | collective-permute-start | bytes 1179656 | tf_op jit(solution)/shard_map/ppermute | solution.py:25
  71.3 2.3 %copy-start = (bf16[1536,1536]{1,0:T(8,128)(2,1)S(1)}, bf16[1536,1536]{1,0:T(8,128)(2,1)}, u32[]{:S(2)}) copy-start(bf16[1536,1536]{1,0:T(8,128)(2,1)} %factor_ref.1) | copy-start | bytes 14155780
  73.6 2.3 %copy-start.1 = (bf16[1536,1536]{0,1:T(8,128)(2,1)S(1)}, bf16[1536,1536]{0,1:T(8,128)(2,1)}, u32[]{:S(2)}) copy-start(bf16[1536,1536]{0,1:T(8,128)(2,1)} %copy.6) | copy-start | bytes 14155780
  75.9 1.0 %copy-start.4 = (bf16[2,4,4,48,128]{4,3,2,1,0:T(8,128)(2,1)S(1)}, bf16[2,4,4,48,128]{4,3,2,1,0:T(8,128)(2,1)}, u32[]{:S(2)}) copy-start(bf16[2,4,4,48,128]{4,3,2,1,0:T(8,128)(2,1)} %copy-done.3) | copy-start | bytes 1179652
  76.9 1.0 %copy-start.6 = (bf16[2,4,4,48,128]{4,3,2,1,0:T(8,128)(2,1)S(1)}, bf16[2,4,4,48,128]{4,3,2,1,0:T(8,128)(2,1)}, u32[]{:S(2)}) copy-start(bf16[2,4,4,48,128]{4,3,2,1,0:T(8,128)(2,1)} %copy-done.5) | copy-start | bytes 1179652
  82.5 2.2 %copy-start.2 = (f32[1,1,8,4,128,128]{5,4,3,2,1,0:T(8,128)S(1)}, f32[1,1,8,4,128,128]{5,4,3,2,1,0:T(8,128)}, u32[]{:S(2)}) copy-start(f32[1,1,8,4,128,128]{5,4,3,2,1,0:T(8,128)} %param.9) | copy-start | bytes 6291460
  82.5 2.2 %copy-start.9 = (s32[32]{0:T(128)S(1)}, s32[32]{0:T(128)}, u32[]{:S(2)}) copy-start(s32[32]{0:T(128)} %map_ref.3) | copy-start | bytes 388

commit v2 on v1

--- a/solution.py
+++ b/solution.py
@@ -7,9 +7,10 @@
 from jax.experimental.pallas import tpu as pltpu
 from jax.sharding import PartitionSpec as P
 
+
 VMEM = pl.BlockSpec(memory_space=pltpu.VMEM)
 SMEM = pl.BlockSpec(memory_space=pltpu.SMEM)
-ANY = pl.BlockSpec(memory_space=pl.ANY)
+HBM = pl.BlockSpec(memory_space=pltpu.HBM)
 
 
 def room(mebibytes):
@@ -25,31 +26,83 @@
     return lax.ppermute(value, axis, [(i, i ^ mask) for i in range(count)])
 
 
+def hops(count):
+    return sorted(range(1, count), key=lambda n: (bin(n).count("1"), -n))
+
+
 def hypercube(value, axis, count, stride):
     held = [value] + [None] * (count - 1)
-    for q in sorted(range(1, count), key=lambda n: (bin(n).count("1"), -n)):
+    for q in hops(count):
         low = q & -q
         held[q] = swap(held[q ^ low], axis, low * stride)
     return held
 
 
-def split_kernel(count, place_ref, rank_ref, x_ref, *outs):
+def two_way_hypercube(value, axis, count):
+    held = [value] + [None] * (count - 1)
+    for m in hops(count):
+        low, high = m & -m, 1 << (m.bit_length() - 1)
+        if low == high:
+            held[m] = swap(value, axis, m)
+            continue
+        half = value.shape[0] // 2
+        first = swap(held[m ^ low][:half], axis, low)
+        second = swap(held[m ^ high][half:], axis, high)
+        held[m] = jnp.concatenate([first, second])
+    return held
+
+
+def split_kernel(count, place_ref, rank_ref, map_ref, x_ref, *refs):
+    outs, map_out, sem = refs[:count], refs[count], refs[count + 1]
     row, blocks = place_ref[0], x_ref.shape[0]
+    copies = [
+        pltpu.make_async_copy(x_ref.at[:, row ^ m], outs[m].at[:blocks], sem.at[m])
+        for m in range(count)
+    ]
+    for copy in copies:
+        copy.start()
     rank = jnp.full(outs[0].shape[1:], rank_ref[0], jnp.float32).astype(x_ref.dtype)
     for m in range(count):
-        outs[m][:blocks] = x_ref[:, row ^ m]
         outs[m][blocks] = rank
-
-
-def split_rows(place, ranks, x):
+    for g in range(map_out.shape[0]):
+        map_out[g] = map_ref[g]
+    for copy in copies:
+        copy.wait()
+
+
+def split_rows(place, ranks, owner_map, x):
     blocks, count, piece, width = x.shape
     return pl.pallas_call(
         functools.partial(split_kernel, count),
-        out_shape=[pltpu.VMEM((blocks + 1, piece, width), x.dtype)] * count,
-        in_specs=[SMEM, SMEM, VMEM],
-        out_specs=[VMEM] * count,
+        out_shape=[pltpu.VMEM((blocks + 1, piece, width), x.dtype)] * count
+        + [pltpu.SMEM(owner_map.shape, owner_map.dtype)],
+        in_specs=[SMEM, SMEM, SMEM, HBM],
+        out_specs=[VMEM] * count + [SMEM],
+        scratch_shapes=[pltpu.SemaphoreType.DMA((count,))],
         compiler_params=room(8),
-    )(place, ranks, near(x))
+    )(place, ranks, owner_map, x)
+
+
+def fetch_kernel(step, factor_ref, near_ref, turned_ref, sem):
+    copy = pltpu.make_async_copy(factor_ref, near_ref, sem)
+    copy.start()
+    copy.wait()
+    order = near_ref.shape[0]
+    for top in range(0, order, step):
+        for left in range(0, top + step, step):
+            block = near_ref[top : top + step, left : left + step]
+            turned_ref[left : left + step, top : top + step] = block.T
+
+
+def fetch(factor, step):
+    return pl.pallas_call(
+        functools.partial(fetch_kernel, step),
+        out_shape=[pltpu.VMEM(factor.shape, factor.dtype)] * 2,
+        in_specs=[HBM],
+        out_specs=[VMEM] * 2,
+        scratch_shapes=[pltpu.SemaphoreType.DMA],
+        compiler_params=room(16),
+    )(factor)
 
 
 def reorder_kernel(n_row, n_col, place_ref, map_ref, *refs):
@@ -115,9 +168,8 @@
         out[top:end] = both.astype(out.dtype)
 
 
-def solve(place, factor, turned, parts, n_row, n_col, piece):
+def solve(place, factor, turned, parts, n_row, n_col, piece, step):
     order, width = factor.shape[0], parts[0].shape[-1]
-    step = 256 if order % 256 == 0 else order
     if piece % 16:
         stacked = jnp.stack(parts).reshape(n_row, n_col, n_row, piece, width)
         col, row = jnp.arange(n_col)[:, None] ^ place[1], jnp.arange(n_row)[None] ^ place[0]
@@ -130,7 +182,7 @@
         out_specs=VMEM,
         scratch_shapes=[pltpu.VMEM((order, n_row * width), factor.dtype)],
         compiler_params=room(24),
-    )(place, factor, turned, *map(near, parts))
+    )(place, near(factor), near(turned), *map(near, parts))
 
 
 def strip(ref, a, n_row, n_col):
@@ -146,7 +198,7 @@
     )
 
 
-def turn_rows(n_row, n_col, piece, masks, place_ref, both_ref, turned):
+def turn_rows(n_row, piece, masks, place_ref, both_ref, turned):
     if piece % 16:
         turned[...] = both_ref[...]
         return
@@ -159,11 +211,12 @@
             turned[there : there + piece] = both_ref[rows]
 
 
-def gram_first_kernel(n_row, n_col, piece, masks, place_ref, both_ref, *refs):
-    strips, out, turned = refs[:-2], refs[-2], refs[-1]
-    turn_rows(n_row, n_col, piece, masks, place_ref, both_ref, turned)
+def gram_kernel(n_row, n_col, piece, masks, place_ref, both_ref, *refs):
+    strips, before, (out, turned) = refs[: len(masks)], refs[len(masks) : -2], refs[-2:]
+    turn_rows(n_row, piece, masks, place_ref, both_ref, turned)
     for a in range(n_col):
-        out[a] = gram_of(n_row, n_col, a, strips, turned)
+        gram = gram_of(n_row, n_col, a, strips, turned)
+        out[a] = gram + before[0][a] if before else gram
 
 
 def gram_last_kernel(n_row, n_col, piece, masks, place_ref, map_ref, both_ref, first_ref, cores_ref, *refs):
@@ -171,7 +224,7 @@
     out, turned, table = refs[-3:]
     row, col = place_ref[0], place_ref[1]
     width = cores_ref.shape[-1]
-    turn_rows(n_row, n_col, piece, masks, place_ref, both_ref, turned)
+    turn_rows(n_row, piece, masks, place_ref, both_ref, turned)
     for m in range(n_col):
         for n in range(n_row):
             rank = chunks[m][n_row * n_col, n : n + 1].astype(jnp.float32)
@@ -210,16 +263,21 @@
         there = jnp.asarray(masks)[:, None] ^ place[1], jnp.arange(n_row)[None] ^ place[0]
         return whole[there].reshape(-1, total)
 
-    cut = n_col - 2
     height = order // n_col
-    first = pl.pallas_call(
-        functools.partial(gram_first_kernel, n_row, n_col, piece, tuple(range(cut))),
-        out_shape=pltpu.VMEM((n_col, width, total), jnp.float32),
-        in_specs=[SMEM, VMEM] + [VMEM] * cut,
-        out_specs=VMEM,
-        scratch_shapes=[pltpu.VMEM((cut * height, total), both.dtype)],
-        compiler_params=room(16),
-    )(place, near(rows_for(range(cut))), *map(near, strips[:cut]))
+
+    def some(masks, before):
+        return pl.pallas_call(
+            functools.partial(gram_kernel, n_row, n_col, piece, masks),
+            out_shape=pltpu.VMEM((n_col, width, total), jnp.float32),
+            in_specs=[SMEM] + [VMEM] * (1 + len(masks) + len(before)),
+            out_specs=VMEM,
+            scratch_shapes=[pltpu.VMEM((len(masks) * height, total), both.dtype)],
+            compiler_params=room(16),
+        )(place, near(rows_for(masks)), *[near(strips[m]) for m in masks], *map(near, before))
+
+    first = some(tuple(range(n_col - 2)), [])
+    first = some((n_col - 2,), [first])
+    cut = n_col - 1
     return pl.pallas_call(
         functools.partial(gram_last_kernel, n_row, n_col, piece, tuple(range(cut, n_col))),
         out_shape=jax.ShapeDtypeStruct(cores.shape, cores.dtype),
@@ -233,7 +291,7 @@
     )(place, owner_map, near(rows_for(range(cut, n_col))), near(first), cores, *map(near, strips[cut:]), *map(near, chunks))
 
 
-def body(panel_right, factor_inverse, ranks, owner_map, cores):
+def panel_step(panel_right, factor_inverse, ranks, owner_map, cores):
     n_row = lax.axis_size("row")
     n_col = lax.axis_size("col")
     blocks, rows, width = panel_right.shape
@@ -243,28 +301,33 @@
     place = jnp.stack([row, col]).astype(jnp.int32)
     planes = n_col // 2
 
-    parts = split_rows(place, ranks, panel_right.reshape(blocks, n_row, piece, width))
+    *parts, owner_map = split_rows(
+        place, ranks, owner_map, panel_right.reshape(blocks, n_row, piece, width)
+    )
     parts = [parts[0]] + [swap(parts[m], "row", m) for m in range(1, n_row)]
     row_parts, col_parts, rank_rows = reorder(place, owner_map, parts, n_row, n_col)
 
     col_parts = [col_parts[0]] + [swap(col_parts[q], "col", 2 * q) for q in range(1, planes)]
     row_parts = [row_parts[0]] + [swap(row_parts[m], "row", m) for m in range(1, n_row)]
+    order = factor_inverse.shape[0]
+    step = 256 if order % 256 == 0 else order
+    factor, turned = fetch(factor_inverse, step)
+
     mine = jnp.stack([part[0] for part in col_parts])
     theirs = swap(jnp.stack([part[1] for part in col_parts]), "col", 1)
-    col_set = hypercube(jnp.stack([mine, theirs]), "row", n_row, 1)
     row_set = hypercube(jnp.concatenate(row_parts + [rank_rows]), "col", planes, 2)
+    col_set = two_way_hypercube(jnp.stack([mine, theirs]), "row", n_row)
     chunks = []
     for part in row_set:
         chunks += [part, swap(part, "col", 1)]
 
-    turned = lax.optimization_barrier(factor_inverse.T)
-    both = solve(place, factor_inverse, turned, col_set, n_row, n_col, piece)
+    both = solve(place, factor, turned, col_set, n_row, n_col, piece, step)
     return gram_update(place, owner_map, both, cores[0, 0], chunks, n_row, n_col, piece)[None, None]
 
 
 def solution(mesh):
     return jax.shard_map(
-        body,
+        panel_step,
         mesh=mesh,
         in_specs=(
             P("row", "col", None),

time: 87.9 us -> 78.1 us (0.89)
  local copies, waits for them, and re-layouts: 16.6 us -> 2.31 us
  starting transfers between devices: 19.8 us -> 24.3 us
  Pallas kernels: 10.9 us -> 12.4 us
  waiting for transfers between devices: 39.1 us -> 37.8 us
    unnamed x25 -> x12, local copies, waits for them, and re-layouts: 16.5 us -> 2.25 us
    ppermute x20 -> x21, starting transfers between devices: 19.8 us -> 24.3 us  [swap(): return lax.ppermute(value, axis, [(i, i ^ mask) for i in range(count)])]
    pallas_call x1 -> x3, Pallas kernels: 2.15 us -> 4.29 us  [the longest x2 3.2 us: some(): pl.pallas_call(functools.partial(gram_kernel, n_row, n_col, piece, masks)...]
    ppermute x20 -> x21, waiting for transfers between devices: 39.1 us -> 37.8 us  [swap(): return lax.ppermute(value, axis, [(i, i ^ mask) for i in range(count)])]
  transfers between devices with their start and end apart: 20 -> 21, of which waited for: 11 -> 10; matrix products, arithmetic and copies ran while one was open for 8% -> 0% of each run, Pallas kernels for 8% -> 11%
where the time goes in v2:
time: 78.1 us; the launch traced here: 78 us
  waiting for transfers between devices  37.8 us (48%)
  starting transfers between devices  24.3 us (31%)
  Pallas kernels  12.4 us (16%)
  local copies, waits for them, and re-layouts  2.31 us (3%)
  between operations  0.86 us (1%)
    ppermute x21, waiting for transfers between devices, swap(): return lax.ppermute(value, axis, [(i, i ^ mask) for i in range(count)])  37.8 us
    ppermute x21, starting transfers between devices, swap(): return lax.ppermute(value, axis, [(i, i ^ mask) for i in range(count)])  24.3 us
    pallas_call x1, Pallas kernels, solve(): pl.pallas_call(functools.partial(solve_kernel, n_row, n_col, piece, step)...  4.01 us
    pallas_call x2, Pallas kernels, some(): pl.pallas_call(functools.partial(gram_kernel, n_row, n_col, piece, masks)...  3.2 us
    pallas_call x1, Pallas kernels, gram_update(): pl.pallas_call(functools.partial(gram_last_kernel, n_row, n_col, piece, t...  2.47 us
    unnamed x12, local copies, waits for them, and re-layouts  2.25 us
  transfers between devices with their start and end apart: 21, of which 10 were waited for; matrix products, arithmetic and copies ran while one was open for 0% of the time, Pallas kernels for 11%

profile of v2, /device:TPU:0, one launch (start us, length us, event | category | flops | bytes accessed | tf_op | source)
XLA Modules:
  0.0 78.0 jit_solution(2519509052662680544)
XLA Ops:
  0.7 0.1 pad_add_fusion.place_ref
  0.7 0.0 copy-start.2
  0.7 1.0 %copy-done.2 = bf16[8,192,128]{2,1,0:T(8,128)(2,1)S(1)} copy-done((bf16[8,192,128]{2,1,0:T(8,128)(2,1)S(1)}, bf16[8,192,128]{2,1,0:T(8,128)(2,1)}, u32[]{:S(2)}) %copy-start.2) | copy-done | bytes 393240
  1.7 0.0 copy-start.3
  1.7 0.7 copy-done.3
  2.4 0.0 copy-start
  2.4 0.7 shard_map.55
  3.1 3.0 %collective-permute-start = (bf16[9,48,128]{2,1,0:T(8,128)(2,1)S(1)}, bf16[9,48,128]{2,1,0:T(8,128)(2,1)S(1)}, u32[]{:S(2)}, u32[]{:S(2)}) collective-permute-start(bf16[9,48,128]{2,1,0:T(8,128)(2,1)S(1)} %get-tuple-element.25), channel_id=1, source_target_pairs={{0,8},{8,0},{16,24},{24,16},{1,9},{9,1},{17,25},{25,17},{2,10},{10... | collective-permute-start | bytes 331784 | tf_op jit(solution)/shard_map/ppermute | solution.py:26
  6.1 1.5 %collective-permute-start.1 = (bf16[9,48,128]{2,1,0:T(8,128)(2,1)S(1)}, bf16[9,48,128]{2,1,0:T(8,128)(2,1)S(1)}, u32[]{:S(2)}, u32[]{:S(2)}) collective-permute-start(bf16[9,48,128]{2,1,0:T(8,128)(2,1)S(1)} %get-tuple-element.26), channel_id=1, source_target_pairs={{0,16},{8,24},{16,0},{24,8},{1,17},{9,25},{17,1},{25,9},{2,18},{10... | collective-permute-start | bytes 331784 | tf_op jit(solution)/shard_map/ppermute | solution.py:26
  7.6 0.0 collective-permute-start.2
  7.7 1.9 %collective-permute-done.refs_1_ = bf16[9,48,128]{2,1,0:T(8,128)(2,1)S(1)} collective-permute-done((bf16[9,48,128]{2,1,0:T(8,128)(2,1)S(1)}, bf16[9,48,128]{2,1,0:T(8,128)(2,1)S(1)}, u32[]{:S(2)}, u32[]{:S(2)}) %collective-permute-start) | collective-permute-done | bytes 110624 | tf_op jit(solution)/shard_map/ppermute | solution.py:26
  9.5 2.5 %collective-permute-done.1.refs_2_ = bf16[9,48,128]{2,1,0:T(8,128)(2,1)S(1)} collective-permute-done((bf16[9,48,128]{2,1,0:T(8,128)(2,1)S(1)}, bf16[9,48,128]{2,1,0:T(8,128)(2,1)S(1)}, u32[]{:S(2)}, u32[]{:S(2)}) %collective-permute-start.1) | collective-permute-done | bytes 110624 | tf_op jit(solution)/shard_map/ppermute | solution.py:26
  12.0 1.2 %collective-permute-done.2.refs_3_ = bf16[9,48,128]{2,1,0:T(8,128)(2,1)S(1)} collective-permute-done((bf16[9,48,128]{2,1,0:T(8,128)(2,1)S(1)}, bf16[9,48,128]{2,1,0:T(8,128)(2,1)S(1)}, u32[]{:S(2)}, u32[]{:S(2)}) %collective-permute-start.2) | collective-permute-done | bytes 110624 | tf_op jit(solution)/shard_map/ppermute | solution.py:26
  13.3 1.0 %shard_map.57 = (bf16[8,48,128]{2,1,0:T(8,128)(2,1)S(1)}, bf16[8,48,128]{2,1,0:T(8,128)(2,1)S(1)}, bf16[8,48,128]{2,1,0:T(8,128)(2,1)S(1)}, bf16[8,48,128]{2,1,0...) custom-call(s32[2]{0:T(128)S(1)} %pad_add_fusion.place_ref, ...), custom_call_target="tpu_custom_call" | custom-call | tf_op jit(solution)/shard_map/pallas_call | solution.py:133
  14.3 3.7 %collective-permute-start.5 = (bf16[2,4,48,128]{3,2,1,0:T(8,128)(2,1)S(1)}, bf16[2,4,48,128]{3,2,1,0:T(8,128)(2,1)S(1)}, u32[]{:S(2)}, u32[]{:S(2)}) collective-permute-start(bf16[2,4,48,128]{3,2,1,0:T(8,128)(2,1)S(1)} %get-tuple-element.31), channel_id=1, source_target_pairs={{0,6},{1,7},{2,4},{3,5},{4,2},{5,3},{6,0},{7,1},{8,14},{9,15},{10,... | collective-permute-start | bytes 294920 | tf_op jit(solution)/shard_map/ppermute | solution.py:26
  17.9 0.0 collective-permute-start.4
  17.9 0.8 %collective-permute-start.3 = (bf16[2,4,48,128]{3,2,1,0:T(8,128)(2,1)S(1)}, bf16[2,4,48,128]{3,2,1,0:T(8,128)(2,1)S(1)}, u32[]{:S(2)}, u32[]{:S(2)}) collective-permute-start(bf16[2,4,48,128]{3,2,1,0:T(8,128)(2,1)S(1)} %get-tuple-element.29), channel_id=1, source_target_pairs={{0,2},{1,3},{2,0},{3,1},{4,6},{5,7},{6,4},{7,5},{8,10},{9,11},{10,... | collective-permute-start | bytes 294920 | tf_op jit(solution)/shard_map/ppermute | solution.py:26
  18.7 1.0 %collective-permute-start.11 = (bf16[8,48,128]{2,1,0:T(8,128)(2,1)S(1)}, bf16[8,48,128]{2,1,0:T(8,128)(2,1)S(1)}, u32[]{:S(2)}, u32[]{:S(2)}) collective-permute-start(bf16[8,48,128]{2,1,0:T(8,128)(2,1)S(1)} %get-tuple-element.33), channel_id=1, source_target_pairs={{0,8},{8,0},{16,24},{24,16},{1,9},{9,1},{17,25},{25,17},{2,10},{10... | collective-permute-start | bytes 294920 | tf_op jit(solution)/shard_map/ppermute | solution.py:26
  19.8 0.8 %collective-permute-start.12 = (bf16[8,48,128]{2,1,0:T(8,128)(2,1)S(1)}, bf16[8,48,128]{2,1,0:T(8,128)(2,1)S(1)}, u32[]{:S(2)}, u32[]{:S(2)}) collective-permute-start(bf16[8,48,128]{2,1,0:T(8,128)(2,1)S(1)} %get-tuple-element.34), channel_id=1, source_target_pairs={{0,16},{8,24},{16,0},{24,8},{1,17},{9,25},{17,1},{25,9},{2,18},{10... | collective-permute-start | bytes 294920 | tf_op jit(solution)/shard_map/ppermute | solution.py:26
  20.6 0.4 collective-permute-done.5
  21.0 1.5 %collective-permute-start.13 = (bf16[8,48,128]{2,1,0:T(8,128)(2,1)S(1)}, bf16[8,48,128]{2,1,0:T(8,128)(2,1)S(1)}, u32[]{:S(2)}, u32[]{:S(2)}) collective-permute-start(bf16[8,48,128]{2,1,0:T(8,128)(2,1)S(1)} %get-tuple-element.35), channel_id=1, source_target_pairs={{0,24},{8,16},{16,8},{24,0},{1,25},{9,17},{17,9},{25,1},{2,26},{10... | collective-permute-start | bytes 294920 | tf_op jit(solution)/shard_map/ppermute | solution.py:26
  22.4 2.2 %collective-permute-done.4 = bf16[2,4,48,128]{3,2,1,0:T(8,128)(2,1)S(1)} collective-permute-done((bf16[2,4,48,128]{3,2,1,0:T(8,128)(2,1)S(1)}, bf16[2,4,48,128]{3,2,1,0:T(8,128)(2,1)S(1)}, u32[]{:S(2)}, u32[]{:S(2)}) %collective-permute-start.4) | collective-permute-done | bytes 98336 | tf_op jit(solution)/shard_map/ppermute | solution.py:26
  24.7 0.0 collective-permute-done.3
  24.8 0.1 collective-permute-start.6
  24.8 0.0 collective-permute-done.11
  24.9 0.0 collective-permute-done.12
  24.9 1.6 %collective-permute-done.13 = bf16[8,48,128]{2,1,0:T(8,128)(2,1)S(1)} collective-permute-done((bf16[8,48,128]{2,1,0:T(8,128)(2,1)S(1)}, bf16[8,48,128]{2,1,0:T(8,128)(2,1)S(1)}, u32[]{:S(2)}, u32[]{:S(2)}) %collective-permute-start.13) | collective-permute-done | bytes 98336 | tf_op jit(solution)/shard_map/ppermute | solution.py:26
  26.5 4.3 %collective-permute-start.14 = (bf16[33,48,128]{2,1,0:T(8,128)(2,1)S(1)}, bf16[33,48,128]{2,1,0:T(8,128)(2,1)S(1)}, u32[]{:S(2)}, u32[]{:S(2)}) collective-permute-start(bf16[33,48,128]{2,1,0:T(8,128)(2,1)S(1)} %constant_dynamic-update-slice_fusion.refs_0_.refs_1_), channel_id=1, source_target_pairs={{0,4},{1,5},{2,6},{3,7},{4,0},{5,1},{6,2},{7,3},{8,12},{9,13},{10,... | collective-permute-start | bytes 1216520 | tf_op jit(solution)/shard_map/ppermute | solution.py:26
  30.8 0.0 collective-permute-done.6
  30.9 2.0 %collective-permute-start.7 = (bf16[2,4,4,48,128]{4,3,2,1,0:T(8,128)(2,1)S(1)}, bf16[2,4,4,48,128]{4,3,2,1,0:T(8,128)(2,1)S(1)}, u32[]{:S(2)}, u32[]{:S(2)}) collective-permute-start(bf16[2,4,4,48,128]{4,3,2,1,0:T(8,128)(2,1)S(1)} %pad_maximum_fusion.refs_0_), channel_id=1, source_target_pairs={{0,8},{8,0},{16,24},{24,16},{1,9},{9,1},{17,25},{25,17},{2,10},{10... | collective-permute-start | bytes 1179656 | tf_op jit(solution)/shard_map/ppermute | solution.py:26
  32.8 0.0 collective-permute-start.17
  32.8 13.6 %collective-permute-done.14.refs_4_.refs_5_ = bf16[33,48,128]{2,1,0:T(8,128)(2,1)S(1)} collective-permute-done((bf16[33,48,128]{2,1,0:T(8,128)(2,1)S(1)}, bf16[33,48,128]{2,1,0:T(8,128)(2,1)S(1)}, u32[]{:S(2)}, u32[]{:S(2)}) %collective-permute-start.14) | collective-permute-done | bytes 405536 | tf_op jit(solution)/shard_map/ppermute | solution.py:26
  46.5 0.0 collective-permute-start.15
  46.5 1.2 %collective-permute-start.8 = (bf16[2,4,4,48,128]{4,3,2,1,0:T(8,128)(2,1)S(1)}, bf16[2,4,4,48,128]{4,3,2,1,0:T(8,128)(2,1)S(1)}, u32[]{:S(2)}, u32[]{:S(2)}) collective-permute-start(bf16[2,4,4,48,128]{4,3,2,1,0:T(8,128)(2,1)S(1)} %pad_maximum_fusion.refs_0_), channel_id=1, source_target_pairs={{0,16},{8,24},{16,0},{24,8},{1,17},{9,25},{17,1},{25,9},{2,18},{10... | collective-permute-start | bytes 1179656 | tf_op jit(solution)/shard_map/ppermute | solution.py:26
  47.7 0.0 collective-permute-done.7.refs_1_
  47.7 0.9 %collective-permute-start.10 = (bf16[1,4,4,48,128]{4,3,2,1,0:T(8,128)(2,1)S(1)}, bf16[1,4,4,48,128]{4,3,2,1,0:T(8,128)(2,1)S(1)}, u32[]{:S(2)}, u32[]{:S(2)}) collective-permute-start(bf16[1,4,4,48,128]{4,3,2,1,0:T(8,128)(2,1)S(1)} %slice.47), channel_id=1, source_target_pairs={{0,16},{8,24},{16,0},{24,8},{1,17},{9,25},{17,1},{25,9},{2,18},{10... | collective-permute-start | bytes 589832 | tf_op jit(solution)/shard_map/ppermute | solution.py:26
  48.6 0.0 collective-permute-start.16
  48.6 0.0 collective-permute-done.17.refs_2_.refs_3_
  48.6 0.5 collective-permute-start.18
  49.1 9.4 %collective-permute-done.8.refs_2_ = bf16[2,4,4,48,128]{4,3,2,1,0:T(8,128)(2,1)S(1)} collective-permute-done((bf16[2,4,4,48,128]{4,3,2,1,0:T(8,128)(2,1)S(1)}, bf16[2,4,4,48,128]{4,3,2,1,0:T(8,128)(2,1)S(1)}, u32[]{:S(2)}, u32[]{:S(2)}) %collective-permute-start.8) | collective-permute-done | bytes 393248 | tf_op jit(solution)/shard_map/ppermute | solution.py:26
  58.5 0.0 collective-permute-start.19
  58.5 0.0 collective-permute-done.15.refs_0_.refs_7_
  58.5 0.5 collective-permute-start.20
  59.0 1.9 %collective-permute-done.10 = bf16[1,4,4,48,128]{4,3,2,1,0:T(8,128)(2,1)S(1)} collective-permute-done((bf16[1,4,4,48,128]{4,3,2,1,0:T(8,128)(2,1)S(1)}, bf16[1,4,4,48,128]{4,3,2,1,0:T(8,128)(2,1)S(1)}, u32[]{:S(2)}, u32[]{:S(2)}) %collective-permute-start.10) | collective-permute-done | bytes 196640 | tf_op jit(solution)/shard_map/ppermute | solution.py:26
  60.9 2.5 %collective-permute-start.9 = (bf16[1,4,4,48,128]{4,3,2,1,0:T(8,128)(2,1)S(1)}, bf16[1,4,4,48,128]{4,3,2,1,0:T(8,128)(2,1)S(1)}, u32[]{:S(2)}, u32[]{:S(2)}) collective-permute-start(bf16[1,4,4,48,128]{4,3,2,1,0:T(8,128)(2,1)S(1)} %slice.46), channel_id=1, source_target_pairs={{0,8},{8,0},{16,24},{24,16},{1,9},{9,1},{17,25},{25,17},{2,10},{10... | collective-permute-start | bytes 589832 | tf_op jit(solution)/shard_map/ppermute | solution.py:26
  63.4 0.0 copy-done
  63.4 1.1 %shard_map.56 = (bf16[1536,1536]{1,0:T(8,128)(2,1)S(1)}, bf16[1536,1536]{1,0:T(8,128)(2,1)S(1)}) custom-call(bf16[1536,1536]{1,0:T(8,128)(2,1)S(1)} %copy-done), custom_call_target="tpu_custom_call" | custom-call | tf_op jit(solution)/shard_map/pallas_call | solution.py:98
  64.5 3.1 %collective-permute-done.9 = bf16[1,4,4,48,128]{4,3,2,1,0:T(8,128)(2,1)S(1)} collective-permute-done((bf16[1,4,4,48,128]{4,3,2,1,0:T(8,128)(2,1)S(1)}, bf16[1,4,4,48,128]{4,3,2,1,0:T(8,128)(2,1)S(1)}, u32[]{:S(2)}, u32[]{:S(2)}) %collective-permute-start.9) | collective-permute-done | bytes 196640 | tf_op jit(solution)/shard_map/ppermute | solution.py:26
  67.7 4.0 %shard_map.58.both_ref = bf16[1536,512]{1,0:T(8,128)(2,1)S(1)} custom-call(s32[2]{0:T(128)S(1)} %pad_add_fusion.place_ref, bf16[1536,1536]{1,0:T(8,128)(2,1)S(1)} %get-tuple-element.22.factor_ref, bf16[1536,1536]{1,0:T(8,128)(2,1)S(1)} %get-tuple-element.23.turned_ref, bf16[2,4,4,48,128]{4,3,2,1,0:T(8,128)(2,1)S(1)} %pad_maximum_fusion.refs_0_, ...), custom_call_target="tpu_custom_call" | custom-call | tf_op jit(solution)/shard_map/pallas_call | solution.py:178
  71.7 0.0 collective-permute-done.16.refs_1_.refs_2_
  71.7 0.0 collective-permute-done.18.refs_3_.refs_4_
  71.7 0.0 collective-permute-done.19.refs_5_.refs_6_
  71.7 2.2 %shard_map.59.refs_1_ = f32[8,128,512]{2,1,0:T(8,128)S(1)} custom-call(s32[2]{0:T(128)S(1)} %pad_add_fusion.place_ref, bf16[1536,512]{1,0:T(8,128)(2,1)S(1)} %shard_map.58.both_ref, bf16[33,48,128]{2,1,0:T(8,128)(2,1)S(1)} %constant_dynamic-update-slice_fusion.refs_0_.refs_1_, bf16[33,48,128]{2,1,0:T(8,128)(2,1)S(1)} %collective-permute-done.16.refs_1_.refs_2_, ...), custom_call_target="tpu_custom_call" | custom-call | tf_op jit(solution)/shard_map/pallas_call | solution.py:269
  73.9 0.0 copy-start.1
  73.9 1.0 %shard_map.60.first_ref = f32[8,128,512]{2,1,0:T(8,128)S(1)} custom-call(s32[2]{0:T(128)S(1)} %pad_add_fusion.place_ref, bf16[1536,512]{1,0:T(8,128)(2,1)S(1)} %shard_map.58.both_ref, bf16[33,48,128]{2,1,0:T(8,128)(2,1)S(1)} %collective-permute-done.15.refs_0_.refs_7_, f32[8,128,512]{2,1,0:T(8,128)S(1)} %shard_map.59.refs_1_), custom_call_target="tpu_custom_call" | custom-call | tf_op jit(solution)/shard_map/pallas_call | solution.py:269
  74.9 0.0 collective-permute-done.20.refs_0_.refs_8_
  74.9 0.5 copy-done.1
  75.5 2.5 %shard_map.61 = f32[8,4,128,128]{3,2,1,0:T(8,128)} custom-call(s32[2]{0:T(128)S(1)} %pad_add_fusion.place_ref, s32[32]{0:T(128)S(4)} %get-tuple-element.21.map_ref, bf16[1536,512]{1,0:T(8,128)(2,1)S(1)} %shard_map.58.both_ref, f32[8,128,512]{2,1,0:T(8,128)S(1)} %shard_map.60.first_ref, f32[8,4,128,128]{3,2,1,0:T(8,128)S(1)} %bitcast.8, ...), custom_call_target="tpu_custom_call" | custom-call | tf_op jit(solution)/shard_map/pallas_call | solution.py:281
  (15 shorter events, 0.3 us)
Async XLA Ops:
  0.7 1.0 %copy-start.2 = (bf16[8,192,128]{2,1,0:T(8,128)(2,1)S(1)}, bf16[8,192,128]{2,1,0:T(8,128)(2,1)}, u32[]{:S(2)}) copy-start(bf16[8,192,128]{2,1,0:T(8,128)(2,1)} %param.5) | copy-start | bytes 1179652
  1.7 0.7 copy-start.3
  2.4 61.0 %copy-start = (bf16[1536,1536]{1,0:T(8,128)(2,1)S(1)}, bf16[1536,1536]{1,0:T(8,128)(2,1)}, u32[]{:S(2)}) copy-start(bf16[1536,1536]{1,0:T(8,128)(2,1)} %factor_ref.1) | copy-start | bytes 14155780
  3.1 6.5 %collective-permute-start = (bf16[9,48,128]{2,1,0:T(8,128)(2,1)S(1)}, bf16[9,48,128]{2,1,0:T(8,128)(2,1)S(1)}, u32[]{:S(2)}, u32[]{:S(2)}) collective-permute-start(bf16[9,48,128]{2,1,0:T(8,128)(2,1)S(1)} %get-tuple-element.25), channel_id=1, source_target_pairs={{0,8},{8,0},{16,24},{24,16},{1,9},{9,1},{17,25},{25,17},{2,10},{10... | collective-permute-start | bytes 331784 | tf_op jit(solution)/shard_map/ppermute | solution.py:26
  6.1 5.9 %collective-permute-start.1 = (bf16[9,48,128]{2,1,0:T(8,128)(2,1)S(1)}, bf16[9,48,128]{2,1,0:T(8,128)(2,1)S(1)}, u32[]{:S(2)}, u32[]{:S(2)}) collective-permute-start(bf16[9,48,128]{2,1,0:T(8,128)(2,1)S(1)} %get-tuple-element.26), channel_id=1, source_target_pairs={{0,16},{8,24},{16,0},{24,8},{1,17},{9,25},{17,1},{25,9},{2,18},{10... | collective-permute-start | bytes 331784 | tf_op jit(solution)/shard_map/ppermute | solution.py:26
  7.6 5.6 %collective-permute-start.2 = (bf16[9,48,128]{2,1,0:T(8,128)(2,1)S(1)}, bf16[9,48,128]{2,1,0:T(8,128)(2,1)S(1)}, u32[]{:S(2)}, u32[]{:S(2)}) collective-permute-start(bf16[9,48,128]{2,1,0:T(8,128)(2,1)S(1)} %get-tuple-element.27), channel_id=1, source_target_pairs={{0,24},{8,16},{16,8},{24,0},{1,25},{9,17},{17,9},{25,1},{2,26},{10... | collective-permute-start | bytes 331784 | tf_op jit(solution)/shard_map/ppermute | solution.py:26
  14.3 6.7 %collective-permute-start.5 = (bf16[2,4,48,128]{3,2,1,0:T(8,128)(2,1)S(1)}, bf16[2,4,48,128]{3,2,1,0:T(8,128)(2,1)S(1)}, u32[]{:S(2)}, u32[]{:S(2)}) collective-permute-start(bf16[2,4,48,128]{3,2,1,0:T(8,128)(2,1)S(1)} %get-tuple-element.31), channel_id=1, source_target_pairs={{0,6},{1,7},{2,4},{3,5},{4,2},{5,3},{6,0},{7,1},{8,14},{9,15},{10,... | collective-permute-start | bytes 294920 | tf_op jit(solution)/shard_map/ppermute | solution.py:26
  17.9 6.7 %collective-permute-start.4 = (bf16[2,4,48,128]{3,2,1,0:T(8,128)(2,1)S(1)}, bf16[2,4,48,128]{3,2,1,0:T(8,128)(2,1)S(1)}, u32[]{:S(2)}, u32[]{:S(2)}) collective-permute-start(bf16[2,4,48,128]{3,2,1,0:T(8,128)(2,1)S(1)} %get-tuple-element.30), channel_id=1, source_target_pairs={{0,4},{1,5},{2,6},{3,7},{4,0},{5,1},{6,2},{7,3},{8,12},{9,13},{10,... | collective-permute-start | bytes 294920 | tf_op jit(solution)/shard_map/ppermute | solution.py:26
  17.9 6.8 %collective-permute-start.3 = (bf16[2,4,48,128]{3,2,1,0:T(8,128)(2,1)S(1)}, bf16[2,4,48,128]{3,2,1,0:T(8,128)(2,1)S(1)}, u32[]{:S(2)}, u32[]{:S(2)}) collective-permute-start(bf16[2,4,48,128]{3,2,1,0:T(8,128)(2,1)S(1)} %get-tuple-element.29), channel_id=1, source_target_pairs={{0,2},{1,3},{2,0},{3,1},{4,6},{5,7},{6,4},{7,5},{8,10},{9,11},{10,... | collective-permute-start | bytes 294920 | tf_op jit(solution)/shard_map/ppermute | solution.py:26
  18.7 6.1 %collective-permute-start.11 = (bf16[8,48,128]{2,1,0:T(8,128)(2,1)S(1)}, bf16[8,48,128]{2,1,0:T(8,128)(2,1)S(1)}, u32[]{:S(2)}, u32[]{:S(2)}) collective-permute-start(bf16[8,48,128]{2,1,0:T(8,128)(2,1)S(1)} %get-tuple-element.33), channel_id=1, source_target_pairs={{0,8},{8,0},{16,24},{24,16},{1,9},{9,1},{17,25},{25,17},{2,10},{10... | collective-permute-start | bytes 294920 | tf_op jit(solution)/shard_map/ppermute | solution.py:26
  19.8 5.1 %collective-permute-start.12 = (bf16[8,48,128]{2,1,0:T(8,128)(2,1)S(1)}, bf16[8,48,128]{2,1,0:T(8,128)(2,1)S(1)}, u32[]{:S(2)}, u32[]{:S(2)}) collective-permute-start(bf16[8,48,128]{2,1,0:T(8,128)(2,1)S(1)} %get-tuple-element.34), channel_id=1, source_target_pairs={{0,16},{8,24},{16,0},{24,8},{1,17},{9,25},{17,1},{25,9},{2,18},{10... | collective-permute-start | bytes 294920 | tf_op jit(solution)/shard_map/ppermute | solution.py:26
  21.0 5.5 %collective-permute-start.13 = (bf16[8,48,128]{2,1,0:T(8,128)(2,1)S(1)}, bf16[8,48,128]{2,1,0:T(8,128)(2,1)S(1)}, u32[]{:S(2)}, u32[]{:S(2)}) collective-permute-start(bf16[8,48,128]{2,1,0:T(8,128)(2,1)S(1)} %get-tuple-element.35), channel_id=1, source_target_pairs={{0,24},{8,16},{16,8},{24,0},{1,25},{9,17},{17,9},{25,1},{2,26},{10... | collective-permute-start | bytes 294920 | tf_op jit(solution)/shard_map/ppermute | solution.py:26
  24.8 6.0 %collective-permute-start.6 = (bf16[4,4,48,128]{3,2,1,0:T(8,128)(2,1)S(1)}, bf16[4,4,48,128]{3,2,1,0:T(8,128)(2,1)S(1)}, u32[]{:S(2)}, u32[]{:S(2)}) collective-permute-start(bf16[4,4,48,128]{3,2,1,0:T(8,128)(2,1)S(1)} %pad_maximum_fusion.2), channel_id=1, source_target_pairs={{0,1},{1,0},{2,3},{3,2},{4,5},{5,4},{6,7},{7,6},{8,9},{9,8},{10,11... | collective-permute-start | bytes 589832 | tf_op jit(solution)/shard_map/ppermute | solution.py:26
  26.5 20.0 %collective-permute-start.14 = (bf16[33,48,128]{2,1,0:T(8,128)(2,1)S(1)}, bf16[33,48,128]{2,1,0:T(8,128)(2,1)S(1)}, u32[]{:S(2)}, u32[]{:S(2)}) collective-permute-start(bf16[33,48,128]{2,1,0:T(8,128)(2,1)S(1)} %constant_dynamic-update-slice_fusion.refs_0_.refs_1_), channel_id=1, source_target_pairs={{0,4},{1,5},{2,6},{3,7},{4,0},{5,1},{6,2},{7,3},{8,12},{9,13},{10,... | collective-permute-start | bytes 1216520 | tf_op jit(solution)/shard_map/ppermute | solution.py:26
  30.9 16.9 %collective-permute-start.7 = (bf16[2,4,4,48,128]{4,3,2,1,0:T(8,128)(2,1)S(1)}, bf16[2,4,4,48,128]{4,3,2,1,0:T(8,128)(2,1)S(1)}, u32[]{:S(2)}, u32[]{:S(2)}) collective-permute-start(bf16[2,4,4,48,128]{4,3,2,1,0:T(8,128)(2,1)S(1)} %pad_maximum_fusion.refs_0_), channel_id=1, source_target_pairs={{0,8},{8,0},{16,24},{24,16},{1,9},{9,1},{17,25},{25,17},{2,10},{10... | collective-permute-start | bytes 1179656 | tf_op jit(solution)/shard_map/ppermute | solution.py:26
  32.8 15.8 %collective-permute-start.17 = (bf16[33,48,128]{2,1,0:T(8,128)(2,1)S(1)}, bf16[33,48,128]{2,1,0:T(8,128)(2,1)S(1)}, u32[]{:S(2)}, u32[]{:S(2)}) collective-permute-start(bf16[33,48,128]{2,1,0:T(8,128)(2,1)S(1)} %constant_dynamic-update-slice_fusion.refs_0_.refs_1_), channel_id=1, source_target_pairs={{0,2},{1,3},{2,0},{3,1},{4,6},{5,7},{6,4},{7,5},{8,10},{9,11},{10,... | collective-permute-start | bytes 1216520 | tf_op jit(solution)/shard_map/ppermute | solution.py:26
  46.5 12.0 %collective-permute-start.15 = (bf16[33,48,128]{2,1,0:T(8,128)(2,1)S(1)}, bf16[33,48,128]{2,1,0:T(8,128)(2,1)S(1)}, u32[]{:S(2)}, u32[]{:S(2)}) collective-permute-start(bf16[33,48,128]{2,1,0:T(8,128)(2,1)S(1)} %collective-permute-done.14.refs_4_.refs_5_), channel_id=1, source_target_pairs={{0,2},{1,3},{2,0},{3,1},{4,6},{5,7},{6,4},{7,5},{8,10},{9,11},{10,... | collective-permute-start | bytes 1216520 | tf_op jit(solution)/shard_map/ppermute | solution.py:26
  46.5 12.0 %collective-permute-start.8 = (bf16[2,4,4,48,128]{4,3,2,1,0:T(8,128)(2,1)S(1)}, bf16[2,4,4,48,128]{4,3,2,1,0:T(8,128)(2,1)S(1)}, u32[]{:S(2)}, u32[]{:S(2)}) collective-permute-start(bf16[2,4,4,48,128]{4,3,2,1,0:T(8,128)(2,1)S(1)} %pad_maximum_fusion.refs_0_), channel_id=1, source_target_pairs={{0,16},{8,24},{16,0},{24,8},{1,17},{9,25},{17,1},{25,9},{2,18},{10... | collective-permute-start | bytes 1179656 | tf_op jit(solution)/shard_map/ppermute | solution.py:26
  47.7 13.1 %collective-permute-start.10 = (bf16[1,4,4,48,128]{4,3,2,1,0:T(8,128)(2,1)S(1)}, bf16[1,4,4,48,128]{4,3,2,1,0:T(8,128)(2,1)S(1)}, u32[]{:S(2)}, u32[]{:S(2)}) collective-permute-start(bf16[1,4,4,48,128]{4,3,2,1,0:T(8,128)(2,1)S(1)} %slice.47), channel_id=1, source_target_pairs={{0,16},{8,24},{16,0},{24,8},{1,17},{9,25},{17,1},{25,9},{2,18},{10... | collective-permute-start | bytes 589832 | tf_op jit(solution)/shard_map/ppermute | solution.py:26
  48.6 23.1 %collective-permute-start.16 = (bf16[33,48,128]{2,1,0:T(8,128)(2,1)S(1)}, bf16[33,48,128]{2,1,0:T(8,128)(2,1)S(1)}, u32[]{:S(2)}, u32[]{:S(2)}) collective-permute-start(bf16[33,48,128]{2,1,0:T(8,128)(2,1)S(1)} %constant_dynamic-update-slice_fusion.refs_0_.refs_1_), channel_id=1, source_target_pairs={{0,1},{1,0},{2,3},{3,2},{4,5},{5,4},{6,7},{7,6},{8,9},{9,8},{10,11... | collective-permute-start | bytes 1216520 | tf_op jit(solution)/shard_map/ppermute | solution.py:26
  48.6 23.1 %collective-permute-start.18 = (bf16[33,48,128]{2,1,0:T(8,128)(2,1)S(1)}, bf16[33,48,128]{2,1,0:T(8,128)(2,1)S(1)}, u32[]{:S(2)}, u32[]{:S(2)}) collective-permute-start(bf16[33,48,128]{2,1,0:T(8,128)(2,1)S(1)} %collective-permute-done.17.refs_2_.refs_3_), channel_id=1, source_target_pairs={{0,1},{1,0},{2,3},{3,2},{4,5},{5,4},{6,7},{7,6},{8,9},{9,8},{10,11... | collective-permute-start | bytes 1216520 | tf_op jit(solution)/shard_map/ppermute | solution.py:26
  58.5 13.2 %collective-permute-start.19 = (bf16[33,48,128]{2,1,0:T(8,128)(2,1)S(1)}, bf16[33,48,128]{2,1,0:T(8,128)(2,1)S(1)}, u32[]{:S(2)}, u32[]{:S(2)}) collective-permute-start(bf16[33,48,128]{2,1,0:T(8,128)(2,1)S(1)} %collective-permute-done.14.refs_4_.refs_5_), channel_id=1, source_target_pairs={{0,1},{1,0},{2,3},{3,2},{4,5},{5,4},{6,7},{7,6},{8,9},{9,8},{10,11... | collective-permute-start | bytes 1216520 | tf_op jit(solution)/shard_map/ppermute | solution.py:26
  58.5 16.5 %collective-permute-start.20 = (bf16[33,48,128]{2,1,0:T(8,128)(2,1)S(1)}, bf16[33,48,128]{2,1,0:T(8,128)(2,1)S(1)}, u32[]{:S(2)}, u32[]{:S(2)}) collective-permute-start(bf16[33,48,128]{2,1,0:T(8,128)(2,1)S(1)} %collective-permute-done.15.refs_0_.refs_7_), channel_id=1, source_target_pairs={{0,1},{1,0},{2,3},{3,2},{4,5},{5,4},{6,7},{7,6},{8,9},{9,8},{10,11... | collective-permute-start | bytes 1216520 | tf_op jit(solution)/shard_map/ppermute | solution.py:26
  60.9 6.8 %collective-permute-start.9 = (bf16[1,4,4,48,128]{4,3,2,1,0:T(8,128)(2,1)S(1)}, bf16[1,4,4,48,128]{4,3,2,1,0:T(8,128)(2,1)S(1)}, u32[]{:S(2)}, u32[]{:S(2)}) collective-permute-start(bf16[1,4,4,48,128]{4,3,2,1,0:T(8,128)(2,1)S(1)} %slice.46), channel_id=1, source_target_pairs={{0,8},{8,0},{16,24},{24,16},{1,9},{9,1},{17,25},{25,17},{2,10},{10... | collective-permute-start | bytes 589832 | tf_op jit(solution)/shard_map/ppermute | solution.py:26
  73.9 1.6 %copy-start.1 = (f32[1,1,8,4,128,128]{5,4,3,2,1,0:T(8,128)S(1)}, f32[1,1,8,4,128,128]{5,4,3,2,1,0:T(8,128)}, u32[]{:S(2)}) copy-start(f32[1,1,8,4,128,128]{5,4,3,2,1,0:T(8,128)} %param.9) | copy-start | bytes 6291460
